TPU v7x, 32 devices: a whole 2x2x4 slice. The times are simulated.
32 devices in a mesh: lat: 16 (over z, y, core), rad: 2 (over x).
Axes of the slice: x: 2, y: 2, z: 4, core: 2. Of those that a mesh axis runs over, the one named last changes fastest.
Arguments:
- displacement: float32 [256, 8, 2048], P('lat', 'rad'), may hold values from -3 to 3
- memory: float32 [256, 8, 2048], P('lat', 'rad'), may hold values from -3 to 3
- ice_class: int32 [256, 2048], P('lat'), may hold values from 0 to 7
- material: int32 [256, 8], P('lat', 'rad'), may hold values from 0 to 7
- mu_table: float32 [8], replicated, may hold values from 0.5 to 4
- decay_table: float32 [8], replicated, may hold values from 0.2 to 0.95
- contrast_table: float32 [8], replicated, may hold values from 0.5 to 2
- gravity_kernel: float32 [256, 8, 8], P('lat', 'rad'), may hold values from -2 to 2
Outputs:
- displacement_out: float32 [256, 8, 2048], P('lat', 'rad')
- memory_out: float32 [256, 8, 2048], P('lat', 'rad')
- potential: float32 [256, 8, 2048], P('lat', 'rad')
All inputs are finite; a program needn't handle non-finite values.
Results may differ from a plain program's by a relative error of at most 0.0028.
Values sent between devices are 32-bit elements; how exact they have to be, the bound alone decides.
A program may use at most 64 MiB of HBM per device.

v0:
```python
import jax
import jax.numpy as jnp
import numpy as np
from jax import lax
from jax.experimental import pallas as pl
from jax.experimental.pallas import tpu as pltpu
from jax.sharding import PartitionSpec as P

MODES = 256


load_scale = 0.5
kappa_shift = 0.5
relax_factor = 0.8
coupling = 2.0
HIGH = lax.Precision.HIGH


def lookup(material, table):
    onehot = (
        material[:, :, None] == jnp.arange(table.shape[0], dtype=jnp.int32)[None, None, :]
    ).astype(jnp.float32)
    return jnp.sum(onehot * table[None, None, :], axis=-1)


def fourier_parts(nlon, modes, minor=128):
    order = np.arange(modes)
    parts = []
    for place in (np.arange(nlon // minor) * minor, np.arange(minor)):
        angle = (place[:, None] * order[None, :] % nlon) * (2.0 * np.pi / nlon)
        parts += [np.cos(angle), np.sin(angle)]
    scale = np.sqrt(2.0 / nlon)
    return [(part * f).astype(np.float32) for part, f in zip(parts, (scale, scale, 1.0, 1.0))]


def fourier_table(nlon, modes):
    ca, sa, cb, sb = lax.optimization_barrier([jnp.asarray(p) for p in fourier_parts(nlon, modes)])
    ca, sa, cb, sb = ca[:, None], sa[:, None], cb[None], sb[None]
    cos = (ca * cb - sa * sb).reshape(nlon, modes)
    sin = (sa * cb + ca * sb).reshape(nlon, modes)
    return jnp.concatenate([cos, sin], axis=1)


def legendre(lat, degrees):
    theta = np.pi * (np.arange(lat) + 0.5) / lat
    cosine = np.cos(theta)
    before, current, rows = np.zeros(lat), np.ones(lat), []
    for n in range(degrees):
        rows.append(current * np.sqrt(n + 0.5))
        before, current = current, ((2.0 * n + 1.0) * cosine * current - n * before) / (n + 1.0)
    basis = np.stack(rows)
    weighted = basis * (np.pi / lat * np.sin(theta))[None, :]
    return basis, weighted


def sweeps_kernel(steps, gather, *refs):
    if gather:
        f_ref, m_ref, s_ref, stiff_ref, decay_ref, g_ref, f_out, m_out, g_out, *refs = refs
        f_buf, face, lat_in, rad_in, send, recv, g_in, g_send, g_recv = refs
    else:
        f_ref, m_ref, s_ref, stiff_ref, decay_ref, f_out, m_out, *refs = refs
        f_buf, face, lat_in, rad_in, send, recv = refs
    layers, rows, nlon = f_ref.shape
    lat_n, rad_n = lax.axis_size("lat"), lax.axis_size("rad")
    lat, rad = lax.axis_index("lat"), lax.axis_index("rad")
    north = (lax.rem(lat + lat_n - 1, lat_n), rad)
    south = (lax.rem(lat + 1, lat_n), rad)
    below = (lat, lax.rem(rad + rad_n - 1, rad_n))
    above = (lat, lax.rem(rad + 1, rad_n))
    if gather:
        peers = [(lax.rem(lat + d, lat_n), rad) for d in range(1, lat_n)] + [below, above]
    else:
        peers = [north, south, below, above]
    barrier = pltpu.get_barrier_semaphore()
    for peer in peers:
        pl.semaphore_signal(barrier, inc=1, device_id=peer, device_id_type=pl.DeviceIdType.MESH)
    pl.semaphore_wait(barrier, len(peers))

    def remote(src, dst, send_sem, recv_sem, peer):
        copy = pltpu.make_async_remote_copy(
            src_ref=src, dst_ref=dst, send_sem=send_sem, recv_sem=recv_sem,
            device_id=peer, device_id_type=pl.DeviceIdType.MESH,
        )
        copy.start()
        return copy

    weight = relax_factor / (6.0 + kappa_shift)
    w_north = jnp.where(lat > 0, weight, 0.0)
    w_south = jnp.where(lat < lat_n - 1, weight, 0.0)
    w_below = jnp.where(rad > 0, weight, 0.0)
    w_above = jnp.where(rad < rad_n - 1, weight, 0.0)
    row = lax.broadcasted_iota(jnp.int32, (rows, nlon), 0)
    gathered = []
    for step in range(steps):
        old = f_ref if step == 0 else f_buf.at[step - 1]
        new = f_out if step == steps - 1 else f_buf.at[step]
        old_m = m_ref if step == 0 else m_out
        for r in range(layers):
            face[step, 0, r : r + 1, :] = old[r, 0:1, :]
            face[step, 1, r : r + 1, :] = old[r, rows - 1 : rows, :]
        copies = [
            remote(old.at[0], rad_in.at[step, 1], send.at[step, 0], recv.at[step, 0], below),
            remote(old.at[layers - 1], rad_in.at[step, 0], send.at[step, 1], recv.at[step, 1], above),
            remote(face.at[step, 0], lat_in.at[step, 1], send.at[step, 2], recv.at[step, 2], north),
            remote(face.at[step, 1], lat_in.at[step, 0], send.at[step, 3], recv.at[step, 3], south),
        ]
        if gather and step == 0:
            gathered = [
                remote(g_ref, g_in.at[lat], g_send.at[d], g_recv.at[d], peers[d - 1])
                for d in range(1, lat_n)
            ]
        for r in range(layers):
            f, m = old[r], old_m[r]
            beside = pltpu.roll(f, 1, 1) + pltpu.roll(f, nlon - 1, 1)
            beside += jnp.where(row == 0, 0.0, pltpu.roll(f, 1, 0))
            beside += jnp.where(row == rows - 1, 0.0, pltpu.roll(f, rows - 1, 0))
            if r > 0:
                beside += old[r - 1]
            if r < layers - 1:
                beside += old[r + 1]
            stiff = stiff_ref[r]
            update = (s_ref[r] - m) * (weight / stiff) - relax_factor * f + weight * beside
            new[r] = f + update
            m_out[r] = decay_ref[r] * m + stiff * update
        for copy in copies:
            copy.wait()
        for r, slot, w in ((0, 0, w_below), (layers - 1, 1, w_above)):
            extra = w * rad_in[step, slot]
            new[r] += extra
            m_out[r] += stiff_ref[r] * extra
        for r in range(layers):
            for j, slot, w in ((0, 0, w_north), (rows - 1, 1, w_south)):
                extra = w * lat_in[step, slot, r : r + 1, :]
                new[r, j : j + 1, :] += extra
                m_out[r, j : j + 1, :] += stiff_ref[r, j : j + 1, :] * extra
    if gather:
        for copy in gathered:
            copy.wait()
        g_in[lat] = g_ref[...]
        g_out[...] = g_in[...]


def sweeps(steps, field, memory, source, stiff, decay, gravity=None):
    gather = gravity is not None
    layers, rows, nlon = field.shape
    block = jax.ShapeDtypeStruct(field.shape, jnp.float32)
    operands, out = [field, memory, source, stiff, decay], [block, block]
    dma, f32 = pltpu.SemaphoreType.DMA, jnp.float32
    scratch = [
        pltpu.VMEM((steps - 1, layers, rows, nlon), f32),
        pltpu.VMEM((steps, 2, layers, nlon), f32),
        pltpu.VMEM((steps, 2, layers, nlon), f32),
        pltpu.VMEM((steps, 2, rows, nlon), f32),
        dma((steps, 4)),
        dma((steps, 4)),
    ]
    if gather:
        lat_n = lax.axis_size("lat")
        every = (lat_n,) + gravity.shape
        operands.append(gravity)
        out.append(jax.ShapeDtypeStruct(every, f32))
        scratch += [pltpu.VMEM(every, f32), dma((lat_n,)), dma((lat_n,))]
    vmem = pl.BlockSpec(memory_space=pltpu.VMEM)

    def kernel(*refs):
        sweeps_kernel(steps, gather, *refs)

    return pl.pallas_call(
        kernel,
        out_shape=out,
        in_specs=[vmem] * len(operands),
        out_specs=[vmem] * len(out),
        scratch_shapes=scratch,
        compiler_params=pltpu.CompilerParams(
            collective_id=0 if gather else 1, has_side_effects=True
        ),
    )(*operands)


LANES = 128
CHUNKS = 4
SWEEPS = 3


def split_np(x):
    x = np.asarray(x, np.float32)
    hi = x.astype(jnp.bfloat16)
    return hi, (x - hi.astype(np.float32)).astype(jnp.bfloat16)


def split(x):
    hi = x.astype(jnp.bfloat16)
    return hi, (x - hi.astype(jnp.float32)).astype(jnp.bfloat16)


def dot3(left, right, transposed=False):
    dims = (((1,), (1 if transposed else 0,)), ((), ()))

    def one(a, b):
        return lax.dot_general(a, b, dims, preferred_element_type=jnp.float32)

    return one(left[0], right[0]) + (one(left[0], right[1]) + one(left[1], right[0]))


def radix_tables(nlon, modes):
    quarter, per = nlon // 4, modes // 4
    place = np.arange(quarter)[:, None]

    def waves(k):
        order = k + 4 * np.arange(per)[None, :]
        angle = (place * order % nlon) * (2.0 * np.pi / nlon)
        return np.sqrt(2.0 / nlon) * np.cos(angle), np.sqrt(2.0 / nlon) * np.sin(angle)

    (c0, s0), (c1, s1), (c2, s2), (c3, s3) = (waves(k) for k in range(4))
    even = np.concatenate([c0, s0, c2, s2], axis=1)
    odd = np.concatenate(
        [np.concatenate([c1, s1, c3, s3], axis=1), np.concatenate([-s1, c1, s3, -c3], axis=1)],
        axis=0,
    )
    return even, odd


def column_orders(modes):
    per = np.arange(modes // 4)
    return np.concatenate([k + 4 * per for k in (0, 0, 2, 2, 1, 1, 3, 3)])


def swap_groups(parts, width):
    parts, step = list(parts), 1
    lane = lax.broadcasted_iota(jnp.int32, parts[0].shape, 1)
    while step < len(parts):
        low = (lane // (width * step)) % 2 == 0
        for g in range(len(parts)):
            if (g // step) % 2 == 0:
                a, b = parts[g], parts[g + step]
                parts[g] = jnp.where(low, a, pltpu.roll(b, width * step, 1))
                parts[g + step] = jnp.where(low, pltpu.roll(a, LANES - width * step, 1), b)
        step *= 2
    return parts


def fused_kernel(
    u_ref, m_ref, ice_ref, stiff_ref, decay_ref, mat_ref, grav_ref,
    even_hi, even_lo, odd_hi, odd_lo, fwd_hi, fwd_lo, inv_hi, inv_lo,
    shift_ref, spread_ref, expand_ref, repeat_ref, mu_ref, dec_ref, con_ref,
    u_out, m_out, p_out,
    ubuf, sbuf, x_in, lat_out, lat_in, g_in, mat_in, pack_out, pack_in, ice_out, ice_in,
    back_out, back_in, gexp, par,
    x_send, x_recv, l_send, l_recv, g_send, g_recv, t_send, t_recv,
    a_send, a_recv, i_send, i_recv, b_send, b_recv,
):
    f32 = jnp.float32
    layers, rows, nlon = u_ref.shape
    lat_n, rad_n = lax.axis_size("lat"), lax.axis_size("rad")
    lat, rad = lax.axis_index("lat"), lax.axis_index("rad")
    count = lat_n * rad_n
    me = lat * rad_n + rad
    total_lat, total_rad = lat_n * rows, rad_n * layers
    halves = rows // 8
    width = LANES // (halves * layers)
    tiles = count * width // LANES
    per_tile = LANES // width
    chunk = nlon // CHUNKS
    last = 2 * SWEEPS
    weight = relax_factor / (6.0 + kappa_shift)

    def device(index):
        return (index // rad_n, lax.rem(index, rad_n))

    def peer(d):
        return lax.rem(me + d, count)

    barrier = pltpu.get_barrier_semaphore()

    def greet(d, carry):
        pl.semaphore_signal(
            barrier, inc=1, device_id=device(peer(d)), device_id_type=pl.DeviceIdType.MESH
        )
        return carry

    lax.fori_loop(1, count, greet, 0)

    def remote(src, dst, send_sem, recv_sem, target):
        return pltpu.make_async_remote_copy(
            src_ref=src, dst_ref=dst, send_sem=send_sem, recv_sem=recv_sem,
            device_id=target, device_id_type=pl.DeviceIdType.MESH,
        )

    def to_all(src_of, dst, send_sem, recv_sem):
        def start(d, carry):
            q = peer(d)
            remote(src_of(q), dst.at[me], send_sem.at[d], recv_sem.at[d], device(q)).start()
            return carry

        lax.fori_loop(1, count, start, 0)

    def each(src_of, dst, send_sem, recv_sem, how):
        def wait(d, carry):
            q = peer(d)
            copy = remote(src_of(q), dst.at[me], send_sem.at[d], recv_sem.at[d], device(q))
            copy.wait_recv() if how == "recv" else copy.wait_send()
            return carry

        lax.fori_loop(1, count, wait, 0)

    sides = (
        (0, rad > 0, 0, (lat, jnp.maximum(rad - 1, 0))),
        (1, rad < rad_n - 1, layers - 1, (lat, jnp.minimum(rad + 1, rad_n - 1))),
    )

    def x_copy(s, side, k, r, target):
        cols = pl.ds(k * chunk, chunk)
        return remote(
            ubuf.at[s, r, :, cols], x_in.at[s, 1 - side, :, cols],
            x_send.at[s, side, k], x_recv.at[s, 1 - side, k], target,
        )

    poles = (
        (0, lat > 0, 0, (jnp.maximum(lat - 1, 0), rad)),
        (1, lat < lat_n - 1, rows - 1, (jnp.minimum(lat + 1, lat_n - 1), rad)),
    )

    def lat_copy(s, side, r, target):
        return remote(
            lat_out.at[s, side, r], lat_in.at[s, 1 - side, r],
            l_send.at[s, side, r], l_recv.at[s, 1 - side, r], target,
        )

    def send_lat(s, r):
        for side, there, j, target in poles:
            @pl.when(there)
            def _():
                lat_out[s, side, r] = ubuf[s, r, j : j + 1, :]
                lat_copy(s, side, r, target).start()

    def sweep(s, more):
        row = lax.broadcasted_iota(jnp.int32, (rows, nlon), 0)

        def inner(r):
            for side, there, _, target in poles:
                @pl.when(there)
                def _():
                    lat_copy(s, 1 - side, r, target).wait_recv()

            f, m = ubuf[s, r], m_out[r]
            beside = pltpu.roll(f, 1, 1) + pltpu.roll(f, nlon - 1, 1)
            beside += jnp.where(row == 0, lat_in[s, 0, r], pltpu.roll(f, 1, 0))
            beside += jnp.where(row == rows - 1, lat_in[s, 1, r], pltpu.roll(f, rows - 1, 0))
            if r > 0:
                beside += ubuf[s, r - 1]
            if r < layers - 1:
                beside += ubuf[s, r + 1]
            stiff = stiff_ref[r]
            update = (sbuf[r] - m) * (weight / stiff) - relax_factor * f + weight * beside
            ubuf[s + 1, r] = f + update
            m_out[r] = decay_ref[r] * m + stiff * update

        rest = list(range(1, layers - 1))
        inner(layers - 1)
        inner(0)
        for k in range(CHUNKS):
            for side, there, r, target in sides:
                @pl.when(there)
                def _():
                    cols = slice(k * chunk, (k + 1) * chunk)
                    x_copy(s, 1 - side, k, r, target).wait_recv()
                    extra = weight * x_in[s, side, :, cols]
                    ubuf[s + 1, r, :, cols] += extra
                    m_out[r, :, cols] += stiff_ref[r] * extra
                    if more is True:
                        x_copy(s + 1, side, k, r, target).start()
                    else:
                        @pl.when(more)
                        def _():
                            x_copy(s + 1, side, k, r, target).start()
            if k < len(rest):
                inner(rest[k])

        def faces():
            for r in range(layers):
                send_lat(s + 1, r)

        if more is True:
            faces()
        else:
            pl.when(more)(faces)

    m_out[...] = m_ref[...]
    ubuf[0] = u_ref[...]
    ice = ice_ref[...].astype(f32)
    for r in range(layers):
        pos = (rad * layers + (r + 1)).astype(f32) / total_rad
        sbuf[r] = (load_scale * pos) * ice
    for side, there, _, _ in poles:
        @pl.when(jnp.logical_not(there))
        def _():
            for s in range(last):
                lat_in[s, side] = jnp.zeros(lat_in.shape[2:], f32)
    g_in[me] = grav_ref[...]
    mat_in[me] = mat_ref[...]

    pl.semaphore_wait(barrier, count - 1)
    for k in range(CHUNKS):
        for side, there, r, target in sides:
            @pl.when(there)
            def _():
                x_copy(0, side, k, r, target).start()
    for r in range(layers):
        send_lat(0, r)
    to_all(lambda q: grav_ref, g_in, g_send, g_recv)
    to_all(lambda q: mat_ref, mat_in, t_send, t_recv)

    quarter = nlon // 4
    block = layers * rows

    def piece(a):
        cols = slice(a * quarter, (a + 1) * quarter)
        return jnp.concatenate(
            [
                u_ref[:, :, cols].reshape(block, quarter),
                m_ref[:, :, cols].reshape(block, quarter),
                ice_ref[:, cols].astype(f32),
            ],
            axis=0,
        )

    x0, x1, x2, x3 = (piece(a) for a in range(4))
    half = even_hi.shape[1] // 2
    both, diff = x0 + x2, x1 + x3
    odd = split(jnp.concatenate([x0 - x2, x1 - x3], axis=1))
    spectra = jnp.concatenate(
        [
            dot3(split(both + diff), (even_hi[:, :half], even_lo[:, :half])),
            dot3(split(both - diff), (even_hi[:, half:], even_lo[:, half:])),
            dot3(odd, (odd_hi[...], odd_lo[...])),
        ],
        axis=1,
    )

    parts = []
    for h in range(halves):
        for r in range(layers):
            at = r * rows + 8 * h
            parts.append(
                jnp.concatenate(
                    [
                        spectra[o + at : o + at + 8, t * LANES : (t + 1) * LANES]
                        for t in range(tiles)
                        for o in (0, block)
                    ],
                    axis=0,
                )
            )
    for p, part in enumerate(swap_groups(parts, width)):
        for t in range(tiles):
            pack_out[per_tile * t + p] = part[16 * t : 16 * (t + 1)]
    to_all(lambda q: pack_out.at[q], pack_in, a_send, a_recv)
    pack_in[me] = pack_out[me]

    sub8 = lax.broadcasted_iota(jnp.int32, (8, LANES), 0)
    group8 = lax.broadcasted_iota(jnp.int32, (8, LANES), 1) // width
    for t in range(tiles):
        cols = slice(t * LANES, (t + 1) * LANES)
        x = spectra[2 * block : 2 * block + 8, cols]
        for h in range(1, halves):
            at = 2 * block + 8 * h
            x = jnp.where(rad == h, spectra[at : at + 8, cols], x)
        for step in (1, 2, 4):
            sb, gb = (sub8 // step) % 2, (group8 // step) % 2
            up = pltpu.roll(pltpu.roll(x, 8 - step, 0), width * step, 1)
            down = pltpu.roll(pltpu.roll(x, step, 0), LANES - width * step, 1)
            x = jnp.where(sb == gb, x, jnp.where(gb == 1, up, down))
        for p in range(per_tile):
            ice_out[per_tile * t + p] = x[p : p + 1]
    to_all(lambda q: ice_out.at[q], ice_in, i_send, i_recv)
    ice_in[me] = ice_out[me]

    each(lambda q: grav_ref, g_in, g_send, g_recv, "recv")
    each(lambda q: mat_ref, mat_in, t_send, t_recv, "recv")
    degrees = fwd_hi.shape[0]
    lane = lax.broadcasted_iota(jnp.int32, (degrees, LANES), 1)
    srow = lax.broadcasted_iota(jnp.int32, (degrees, LANES), 0)
    held = LANES // (layers * total_rad)
    cut = lane // (layers * total_rad) == lax.rem(srow, held)
    repeat = repeat_ref[...]
    wide = []
    for x in range(rad_n):
        lines = split(
            jnp.concatenate([g_in[rad_n * i + x] for i in range(lat_n)], axis=0)
        )
        full = jnp.dot(repeat, lines[0], preferred_element_type=f32) + jnp.dot(
            repeat, lines[1], preferred_element_type=f32
        )
        wide.append(jnp.where(cut, full, 0.0))
    wide = split(jnp.concatenate(wide, axis=1))
    for d in range(total_rad):
        cols = slice(d * LANES, (d + 1) * LANES)
        gexp[:, cols] = jnp.dot(
            wide[0], expand_ref[:, cols], preferred_element_type=f32
        ) + jnp.dot(wide[1], expand_ref[:, cols], preferred_element_type=f32)

    jrow = lax.broadcasted_iota(jnp.int32, (rows, LANES), 0)
    jlane = (lax.broadcasted_iota(jnp.int32, (rows, LANES), 1) // layers) % rows
    ids = []
    for i in range(lat_n):
        line = mat_in[rad_n * i]
        for x in range(1, rad_n):
            line = line + mat_in[rad_n * i + x]
        ids.append(jnp.where(jrow == jlane, jnp.broadcast_to(line, (rows, LANES)), 0.0))
    ids = jnp.dot(
        jnp.concatenate(ids, axis=0).astype(jnp.bfloat16), spread_ref[...],
        preferred_element_type=f32,
    )
    for n, table in enumerate((mu_ref, dec_ref, con_ref)):
        value = jnp.zeros((total_lat, LANES), f32)
        for k in range(table.shape[0]):
            value = jnp.where(ids == k, table[k], value)
        par[n] = value

    def two(s, carry):
        sweep(s, True)
        return carry

    lax.fori_loop(0, SWEEPS - 1, two, 0)

    each(lambda q: pack_out.at[q], pack_in, a_send, a_recv, "recv")
    each(lambda q: ice_out.at[q], ice_in, i_send, i_recv, "recv")
    near = lax.broadcasted_iota(jnp.int32, (16, LANES), 1) < LANES // 2
    us, qs, ss = [], [], []
    sub = lax.broadcasted_iota(jnp.int32, (8, LANES), 0)
    for i in range(lat_n):
        a, b = pack_in[rad_n * i], pack_in[rad_n * i + 1]
        top = jnp.where(near, a, pltpu.roll(b, LANES // 2, 1))
        low = jnp.where(near, pltpu.roll(a, LANES // 2, 1), b)
        us += [top[:8], low[:8]]
        qs += [top[8:], low[8:]]
        for x in range(rad_n):
            ss.append(
                jnp.where(sub == group8, jnp.broadcast_to(ice_in[rad_n * i + x], (8, LANES)), 0.0)
            )
    u, q, s_hat = (jnp.concatenate(v, axis=0) for v in (us, qs, ss))
    step = width
    while step < LANES:
        s_hat = s_hat + pltpu.roll(s_hat, step, 1)
        step *= 2
    glane = lax.broadcasted_iota(jnp.int32, (total_lat, LANES), 1)
    grow = lax.broadcasted_iota(jnp.int32, (total_lat, LANES), 0)
    s_hat = s_hat * ((glane // width + 1).astype(f32) * (load_scale / total_rad))
    shift = shift_ref[pl.ds(me, 1), :]
    stiff, decay, contrast = par[0], par[1], par[2]
    scaled = weight / stiff
    for n in range(SWEEPS):
        beside = shift * u
        beside += jnp.where(grow == 0, 0.0, pltpu.roll(u, 1, 0))
        beside += jnp.where(grow == total_lat - 1, 0.0, pltpu.roll(u, total_lat - 1, 0))
        beside += jnp.where(glane < width, 0.0, pltpu.roll(u, width, 1))
        beside += jnp.where(glane >= LANES - width, 0.0, pltpu.roll(u, LANES - width, 1))
        update = (s_hat - q) * scaled - relax_factor * u + weight * beside
        u = u + update
        q = decay * q + stiff * update
    rho = contrast * u
    zero = jnp.logical_and(me == 0, lax.rem(glane, width) == 0)
    mean = jnp.sum(jnp.where(zero, rho, 0.0)) / (total_lat * total_rad)
    rho = rho - jnp.where(zero, mean, 0.0)
    coef = dot3((fwd_hi[...], fwd_lo[...]), split(rho))
    phi = gexp[:, :LANES] * coef
    for d in range(1, total_rad):
        phi += gexp[:, d * LANES : (d + 1) * LANES] * pltpu.roll(coef, width * d, 1)
    synth = dot3((inv_hi[...], inv_lo[...]), split(phi))
    near8 = lax.broadcasted_iota(jnp.int32, (8, LANES), 1) < LANES // 2
    for i in range(lat_n):
        a, b = synth[rows * i : rows * i + 8], synth[rows * i + 8 : rows * i + 16]
        back_out[rad_n * i] = jnp.where(near8, a, pltpu.roll(b, LANES // 2, 1))
        back_out[rad_n * i + 1] = jnp.where(near8, pltpu.roll(a, LANES // 2, 1), b)
    to_all(lambda q: back_out.at[q], back_in, b_send, b_recv)
    back_in[me] = back_out[me]

    sweep(SWEEPS - 1, True)

    each(lambda q: back_out.at[q], back_in, b_send, b_recv, "recv")
    parts = swap_groups(
        [
            jnp.concatenate([back_in[per_tile * t + p] for t in range(tiles)], axis=0)
            for p in range(per_tile)
        ],
        width,
    )
    lines = []
    for r in range(layers):
        for h in range(halves):
            part = parts[h * layers + r]
            lines.append(
                jnp.concatenate([part[8 * t : 8 * (t + 1)] for t in range(tiles)], axis=1)
            )
    z = jnp.concatenate(lines, axis=0)
    y0 = dot3(split(z[:, :half]), (even_hi[:, :half], even_lo[:, :half]), True)
    y2 = dot3(split(z[:, half : 2 * half]), (even_hi[:, half:], even_lo[:, half:]), True)
    y13 = dot3(split(z[:, 2 * half :]), (odd_hi[...], odd_lo[...]), True)
    alpha, beta = y13[:, :quarter], y13[:, quarter:]
    plus, minus = y0 + y2, y0 - y2
    for a, value in enumerate((plus + alpha, minus + beta, plus - alpha, minus - beta)):
        cols = slice(a * quarter, (a + 1) * quarter)
        value = value.reshape(layers, rows, quarter)
        p_out[:, :, cols] = value
        sbuf[:, :, cols] += coupling * value

    def rest(s, carry):
        sweep(s, s + 1 < last)
        return carry

    lax.fori_loop(SWEEPS, last, rest, 0)
    u_out[...] = ubuf[last]

    each(lambda q: grav_ref, g_in, g_send, g_recv, "send")
    each(lambda q: mat_ref, mat_in, t_send, t_recv, "send")
    each(lambda q: pack_out.at[q], pack_in, a_send, a_recv, "send")
    each(lambda q: ice_out.at[q], ice_in, i_send, i_recv, "send")
    each(lambda q: back_out.at[q], back_in, b_send, b_recv, "send")

    def drain(s, carry):
        for side, there, r, target in sides:
            @pl.when(there)
            def _():
                for k in range(CHUNKS):
                    x_copy(s, side, k, r, target).wait_send()
        for side, there, _, target in poles:
            @pl.when(there)
            def _():
                for r in range(layers):
                    lat_copy(s, side, r, target).wait_send()
        return carry

    lax.fori_loop(0, last, drain, 0)


def fused(displacement, memory, ice_class, stiff, decay, material, tables, gravity):
    lat_dev, r_dev, nlon = displacement.shape
    lat_n, rad_n = lax.axis_size("lat"), lax.axis_size("rad")
    count, total_lat, total_rad = lat_n * rad_n, lat_n * lat_dev, rad_n * r_dev
    degrees = gravity.shape[0] * lat_n
    width = 2 * MODES // count
    bf16, f32 = jnp.bfloat16, jnp.float32
    even, odd = (split_np(t) for t in radix_tables(nlon, MODES))
    basis, weighted = legendre(total_lat, degrees)
    fwd, inv = split_np(weighted), split_np(basis.T)
    orders = column_orders(MODES).reshape(count, width)
    shift = np.tile(2.0 * np.cos(2.0 * np.pi * orders / nlon), (1, total_rad)).astype(np.float32)
    spread = np.zeros((LANES, LANES))
    for x in range(rad_n):
        for j in range(lat_dev):
            for r in range(r_dev):
                at = (x * r_dev + r) * width
                spread[x * lat_dev * r_dev + j * r_dev + r, at : at + width] = 1.0
    held = LANES // (r_dev * total_rad)
    expand = np.zeros((rad_n, held, r_dev, total_rad, total_rad, total_rad, width))
    for x in range(rad_n):
        for r in range(r_dev):
            for d in range(total_rad):
                to = x * r_dev + r
                expand[x, :, r, (to - d) % total_rad, d, to, :] = 1.0
    expand = expand.reshape(rad_n * LANES, total_rad * LANES)
    repeat = np.repeat(np.eye(degrees // held), held, axis=0)
    rad = lax.axis_index("rad")
    ids = material.astype(f32).reshape(1, lat_dev * r_dev)
    ids = jnp.concatenate([jnp.where(rad == x, ids, 0.0) for x in range(rad_n)], axis=1)
    gravity = gravity.reshape(-1, LANES)
    lines = gravity.shape[0]
    operands = [
        displacement.transpose(1, 0, 2), memory.transpose(1, 0, 2), ice_class, stiff, decay, ids, gravity,
        *even, *odd, *fwd, *inv, shift,
        spread.astype(bf16), expand.astype(bf16), repeat.astype(bf16), *tables,
    ]
    operands = [jnp.asarray(x) for x in operands]
    vmem = pl.BlockSpec(memory_space=pltpu.VMEM)
    smem = pl.BlockSpec(memory_space=pltpu.SMEM)
    dma = pltpu.SemaphoreType.DMA
    steps = 2 * SWEEPS
    block = jax.ShapeDtypeStruct((r_dev, lat_dev, nlon), f32)
    out = pl.pallas_call(
        fused_kernel,
        out_shape=[block] * 3,
        in_specs=[vmem] * (len(operands) - len(tables)) + [smem] * len(tables),
        out_specs=[vmem] * 3,
        scratch_shapes=[
            pltpu.VMEM((steps + 1, r_dev, lat_dev, nlon), f32),
            pltpu.VMEM((r_dev, lat_dev, nlon), f32),
            pltpu.VMEM((steps, 2, lat_dev, nlon), f32),
            pltpu.VMEM((steps, 2, r_dev, 1, nlon), f32),
            pltpu.VMEM((steps, 2, r_dev, 1, nlon), f32),
            pltpu.VMEM((count, lines, LANES), f32),
            pltpu.VMEM((count, 1, LANES), f32),
            pltpu.VMEM((count, 16, LANES), f32),
            pltpu.VMEM((count, 16, LANES), f32),
            pltpu.VMEM((count, 1, LANES), f32),
            pltpu.VMEM((count, 1, LANES), f32),
            pltpu.VMEM((count, 8, LANES), f32),
            pltpu.VMEM((count, 8, LANES), f32),
            pltpu.VMEM((degrees, total_rad * LANES), f32),
            pltpu.VMEM((3, total_lat, LANES), f32),
            dma((steps, 2, CHUNKS)), dma((steps, 2, CHUNKS)),
            dma((steps, 2, r_dev)), dma((steps, 2, r_dev)),
        ] + [dma((count,))] * 10,
        compiler_params=pltpu.CompilerParams(collective_id=2, has_side_effects=True),
    )(*operands)
    return tuple(x.transpose(1, 0, 2) for x in out)


def fits(lat_dev, r_dev, total_rad, rad_n, count):
    width = 2 * MODES // count
    return (
        rad_n == 2
        and lat_dev == 16
        and width * count == 2 * MODES
        and width * total_rad == LANES
        and rad_n * lat_dev * r_dev == LANES
        and LANES % (r_dev * total_rad) == 0
    )


def per_device(
    displacement, memory, ice_class, material, mu_table, decay_table, contrast_table, gravity_kernel
):
    lat_dev, r_dev, nlon = displacement.shape
    lat_count = lax.axis_size("lat")
    rad_count = lax.axis_size("rad")
    rad_index = lax.axis_index("rad")
    total_lat = lat_count * lat_dev
    total_rad = rad_count * r_dev
    degrees = gravity_kernel.shape[0] * lat_count
    cols = 2 * MODES
    columns = cols // lat_count
    stiff = lookup(material.T, mu_table)[:, :, None]
    decay = lookup(material.T, decay_table)[:, :, None]
    contrast = lookup(material.T, contrast_table)[:, :, None]
    layer_pos = (rad_index * r_dev + jnp.arange(r_dev, dtype=jnp.int32) + 1).astype(
        jnp.float32
    ) / total_rad
    source = load_scale * ice_class.astype(jnp.float32)[None, :, :] * layer_pos[:, None, None]
    if fits(lat_dev, r_dev, total_rad, rad_count, lat_count * rad_count):
        tables = (mu_table, decay_table, contrast_table)
        return fused(
            displacement, memory, ice_class, stiff, decay, material, tables, gravity_kernel
        )
    basis, weighted = legendre(total_lat, degrees)
    projection = jnp.asarray(
        np.concatenate([weighted, np.ones((8, total_lat))]).astype(np.float32)
    )
    weight_sum = jnp.asarray(weighted.sum(axis=1).astype(np.float32))
    basis = jnp.asarray(basis.T.astype(np.float32))
    table = fourier_table(nlon, MODES)
    field, mem, kernel_every = sweeps(
        3,
        displacement.transpose(1, 0, 2),
        memory.transpose(1, 0, 2),
        source,
        stiff,
        decay,
        gravity_kernel.reshape(gravity_kernel.shape[0], -1),
    )
    kernel_every = kernel_every.reshape((degrees,) + gravity_kernel.shape[1:])
    rho = contrast * field
    spectra = jnp.dot(rho.reshape(lat_dev * r_dev, nlon), table, precision=HIGH)
    spread = lax.all_to_all(
        spectra.reshape(r_dev, lat_dev, cols).transpose(1, 0, 2), "lat", split_axis=2, concat_axis=0, tiled=True
    )
    coef_cols = jnp.dot(
        projection, spread.reshape(total_lat, r_dev * columns), precision=HIGH
    ).reshape(degrees + 8, r_dev, columns)
    coef_all = lax.all_gather(coef_cols, "rad", axis=1, tiled=True)
    first_order = (lax.axis_index("lat") * columns + jnp.arange(columns, dtype=jnp.int32)) == 0
    mean_row = jnp.sum(coef_all[degrees], axis=0) / (total_lat * total_rad)
    mean_row = jnp.where(first_order, mean_row, 0.0)
    coef_all = coef_all[:degrees] - weight_sum[:, None, None] * mean_row[None, None, :]
    phi_cols = jnp.sum(kernel_every[:, :, :, None] * coef_all[:, None, :, :], axis=2)
    synth_cols = jnp.dot(
        basis, phi_cols.reshape(degrees, r_dev * columns), precision=HIGH
    ).reshape(total_lat, r_dev, columns)
    synth = lax.all_to_all(synth_cols, "lat", split_axis=0, concat_axis=2, tiled=True)
    potential = lax.dot_general(
        synth.transpose(1, 0, 2).reshape(r_dev * lat_dev, cols), table, (((1,), (1,)), ((), ())), precision=HIGH
    ).reshape(r_dev, lat_dev, nlon)
    loaded = source + coupling * potential
    field, mem = sweeps(3, field, mem, loaded, stiff, decay)
    return tuple(x.transpose(1, 0, 2) for x in (field, mem, potential))


def solution(mesh):
    placed = (
        P("lat", "rad", None),
        P("lat", "rad", None),
        P("lat", None),
        P("lat", "rad"),
        P(),
        P(),
        P(),
        P("lat", "rad", None),
    )
    return jax.shard_map(
        per_device,
        mesh=mesh,
        in_specs=placed,
        out_specs=(P("lat", "rad", None), P("lat", "rad", None), P("lat", "rad", None)),
        check_vma=False,
    )
```

profile of v0, /device:TPU:0, one launch (start us, length us, event | category | flops | bytes accessed | tf_op | source)
XLA Modules:
  0.0 59.1 jit_solution(3550142944353213786)
XLA Ops:
  0.6 0.0 copy-start.3
  0.6 0.7 %copy-done.3 = s32[16,4]{0,1:T(4,128)S(1)} copy-done((s32[16,4]{0,1:T(4,128)S(1)}, s32[16,4]{0,1:T(4,128)}, u32[]{:S(2)}) %copy-start.3) | copy-done | bytes 280
  1.3 0.0 copy-start.4
  1.3 0.0 copy-start.5
  1.3 0.7 %copy-done.4 = f32[8]{0:T(128)S(1)} copy-done((f32[8]{0:T(128)S(1)}, f32[8]{0:T(128)}, u32[]{:S(2)}) %copy-start.4) | copy-done | bytes 56
  2.0 0.0 copy-done.5
  2.0 0.1 select_reduce_fusion
  2.1 0.1 copy.45
  2.2 0.1 select_n.38
  2.3 0.1 copy.46
  2.3 0.1 select_n.41
  2.4 0.6 %pad_maximum_fusion.mat_ref = f32[1,128]{1,0:T(1,128)} fusion(f32[1,64]{1,0:T(1,128)S(1)} %select_n.41, f32[1,64]{1,0:T(1,128)S(1)} %select_n.38), kind=kLoop, calls=%fused_computation.7 | loop fusion | flops 128 | bytes 1024 | tf_op jit(solution)/shard_map/concatenate | solution.py:665
  3.0 0.7 %copy.48.stiff_ref = f32[4,16,1]{2,1,0:T(8,128)} copy(f32[4,16,1]{1,0,2:T(4,128)S(1)} %bitcast.15) | data formatting | bytes 512 | tf_op jit(solution)/shard_map/broadcast_in_dim | solution.py:732
  3.8 0.0 copy-start.2
  3.8 0.7 %copy.49.decay_ref = f32[4,16,1]{2,1,0:T(8,128)} copy(f32[4,16,1]{1,0,2:T(4,128)S(1)} %bitcast.14) | data formatting | bytes 512 | tf_op jit(solution)/shard_map/broadcast_in_dim | solution.py:733
  4.5 0.0 copy-done.2
  4.5 0.1 copy.47
  4.6 0.7 %reshape.43.grav_ref = f32[4,128]{1,0:T(4,128)} reshape(f32[16,4,8]{2,1,0:T(4,128)S(1)} %copy.47) | data formatting | bytes 4096 | tf_op jit(solution)/shard_map/reshape | solution.py:666
  5.2 2.8 %copy_bitcast_fusion = (f32[4,16,2048]{2,1,0:T(8,128)}, f32[4,16,2048]{2,1,0:T(8,128)}) fusion(f32[16,4,2048]{2,1,0:T(4,128)} %param.21, f32[16,4,2048]{2,1,0:T(4,128)} %param.20), kind=kLoop, calls=%fused_computation | loop fusion | bytes 2097152 | tf_op jit(solution)/shard_map/transpose | solution.py:669
  8.0 46.5 %shard_map.211 = (f32[4,16,2048]{2,1,0:T(8,128)}, f32[4,16,2048]{2,1,0:T(8,128)}, f32[4,16,2048]{2,1,0:T(8,128)}) custom-call(f32[4,16,2048]{2,1,0:T(8,128)} %get-tuple-element.23.u_ref, f32[4,16,2048]{2,1,0:T(8,128)} %get-tuple-element.22.m_ref, s32[16,2048]{1,0:T(8,128)} %ice_ref.1, f32[4,16,1]{2,1,0:T(8,128)} %copy.48.stiff_ref, ...), custom_call_target="tpu_custom_call" | custom-call | tf_op jit(solution)/shard_map/pallas_call | solution.py:679
  54.6 0.0 copy-start.1
  54.6 2.2 %copy.50 = f32[16,4,2048]{2,1,0:T(4,128)} copy(f32[16,4,2048]{2,0,1:T(8,128)} %bitcast.12) | data formatting | bytes 1048576
  56.8 0.0 copy-done.1
  56.8 0.0 copy-start
  56.8 1.1 %copy.51 = f32[16,4,2048]{2,1,0:T(4,128)} copy(f32[16,4,2048]{2,0,1:T(8,128)S(1)} %bitcast.11) | data formatting | bytes 1048576
  57.9 0.0 copy-done
  57.9 1.1 %copy.52 = f32[16,4,2048]{2,1,0:T(4,128)} copy(f32[16,4,2048]{2,0,1:T(8,128)S(1)} %bitcast.10) | data formatting | bytes 1048576
  (1 shorter events, 0.0 us)
Async XLA Ops:
  0.6 0.7 %copy-start.3 = (s32[16,4]{0,1:T(4,128)S(1)}, s32[16,4]{0,1:T(4,128)}, u32[]{:S(2)}) copy-start(s32[16,4]{0,1:T(4,128)} %param.23) | copy-start | bytes 772
  1.3 0.7 %copy-start.4 = (f32[8]{0:T(128)S(1)}, f32[8]{0:T(128)}, u32[]{:S(2)}) copy-start(f32[8]{0:T(128)} %dec_ref.1) | copy-start | bytes 100
  1.3 0.7 %copy-start.5 = (f32[8]{0:T(128)S(1)}, f32[8]{0:T(128)}, u32[]{:S(2)}) copy-start(f32[8]{0:T(128)} %mu_ref.1) | copy-start | bytes 100
  3.8 0.7 %copy-start.2 = (f32[16,4,8]{0,2,1:T(8,128)S(1)}, f32[16,4,8]{0,2,1:T(8,128)}, u32[]{:S(2)}) copy-start(f32[16,4,8]{0,2,1:T(8,128)} %param.27) | copy-start | bytes 6148
  54.6 2.2 %copy-start.1 = (f32[4,16,2048]{2,1,0:T(8,128)S(1)}, f32[4,16,2048]{2,1,0:T(8,128)}, u32[]{:S(2)}) copy-start(f32[4,16,2048]{2,1,0:T(8,128)} %get-tuple-element.7) | copy-start | bytes 1572868
  56.8 1.1 %copy-start = (f32[4,16,2048]{2,1,0:T(8,128)S(1)}, f32[4,16,2048]{2,1,0:T(8,128)}, u32[]{:S(2)}) copy-start(f32[4,16,2048]{2,1,0:T(8,128)} %get-tuple-element.8) | copy-start | bytes 1572868
where the time goes:
time: 59.6 us; the launch traced here: 59.1 us
  Pallas kernels  46.5 us (78%)
  local copies, waits for them, and re-layouts  11.2 us (19%)
  other arithmetic  0.71 us (1%)
  between operations  0.68 us (1%)
    pallas_call x1, Pallas kernels, fused(): pl.pallas_call(fused_kernel, out_shape=[block] * 3, in_specs=[vmem] * (le...  46.5 us
    unnamed x16, local copies, waits for them, and re-layouts  5.93 us
    transpose x1, local copies, waits for them, and re-layouts, fused(): memory.transpose(1, 0, 2)  2.77 us

commit v1 on v0

--- a/solution.py
+++ b/solution.py
@@ -240,17 +240,17 @@
 
 
 def fused_kernel(
-    u_ref, m_ref, ice_ref, stiff_ref, decay_ref, mat_ref, grav_ref,
-    even_hi, even_lo, odd_hi, odd_lo, fwd_hi, fwd_lo, inv_hi, inv_lo,
-    shift_ref, spread_ref, expand_ref, repeat_ref, mu_ref, dec_ref, con_ref,
+    u_ref, m_ref, ice_hbm, table_hbm, stiff_ref, decay_ref, mat_ref, grav_ref,
+    shift_ref, mu_ref, dec_ref, con_ref,
     u_out, m_out, p_out,
+    ice_ref, even_hi, even_lo, odd_hi, odd_lo, expand_ref, fwd_hi, fwd_lo, inv_hi, inv_lo, load_sem,
     ubuf, sbuf, x_in, lat_out, lat_in, g_in, mat_in, pack_out, pack_in, ice_out, ice_in,
     back_out, back_in, gexp, par,
     x_send, x_recv, l_send, l_recv, g_send, g_recv, t_send, t_recv,
     a_send, a_recv, i_send, i_recv, b_send, b_recv,
 ):
     f32 = jnp.float32
-    layers, rows, nlon = u_ref.shape
+    rows, layers, nlon = u_ref.shape
     lat_n, rad_n = lax.axis_size("lat"), lax.axis_size("rad")
     lat, rad = lax.axis_index("lat"), lax.axis_index("rad")
     count = lat_n * rad_n
@@ -280,6 +280,18 @@
 
     lax.fori_loop(1, count, greet, 0)
 
+    pairs = [(u_ref.at[:, r, :], ubuf.at[0, r]) for r in range(layers)]
+    pairs += [(m_ref.at[:, r, :], m_out.at[r]) for r in range(layers)]
+    pairs.append((ice_hbm, ice_ref))
+    at = 0
+    for held in (even_hi, even_lo, odd_hi, odd_lo, expand_ref, fwd_hi, fwd_lo, inv_hi, inv_lo):
+        pairs.append((table_hbm.at[pl.ds(at, held.shape[0])], held))
+        at += held.shape[0]
+    loads = [pltpu.make_async_copy(a, b, load_sem.at[n]) for n, (a, b) in enumerate(pairs)]
+    for load in loads:
+        load.start()
+    first = 2 * layers + 1
+
     def remote(src, dst, send_sem, recv_sem, target):
         return pltpu.make_async_remote_copy(
             src_ref=src, dst_ref=dst, send_sem=send_sem, recv_sem=recv_sem,
@@ -335,6 +347,11 @@
 
     def sweep(s, more):
         row = lax.broadcasted_iota(jnp.int32, (rows, nlon), 0)
+
+        def forward(r, when):
+            @pl.when(jnp.logical_and(when, more))
+            def _():
+                send_lat(s + 1, r)
 
         def inner(r):
             for side, there, _, target in poles:
@@ -354,6 +371,11 @@
             update = (sbuf[r] - m) * (weight / stiff) - relax_factor * f + weight * beside
             ubuf[s + 1, r] = f + update
             m_out[r] = decay_ref[r] * m + stiff * update
+            alone = True
+            for side, there, edge, _ in sides:
+                if edge == r:
+                    alone = jnp.logical_not(there)
+            forward(r, alone)
 
         rest = list(range(1, layers - 1))
         inner(layers - 1)
@@ -376,21 +398,9 @@
             if k < len(rest):
                 inner(rest[k])
 
-        def faces():
-            for r in range(layers):
-                send_lat(s + 1, r)
-
-        if more is True:
-            faces()
-        else:
-            pl.when(more)(faces)
-
-    m_out[...] = m_ref[...]
-    ubuf[0] = u_ref[...]
-    ice = ice_ref[...].astype(f32)
-    for r in range(layers):
-        pos = (rad * layers + (r + 1)).astype(f32) / total_rad
-        sbuf[r] = (load_scale * pos) * ice
+        for side, there, r, _ in sides:
+            forward(r, there)
+
     for side, there, _, _ in poles:
         @pl.when(jnp.logical_not(there))
         def _():
@@ -398,17 +408,14 @@
                 lat_in[s, side] = jnp.zeros(lat_in.shape[2:], f32)
     g_in[me] = grav_ref[...]
     mat_in[me] = mat_ref[...]
-
-    pl.semaphore_wait(barrier, count - 1)
-    for k in range(CHUNKS):
-        for side, there, r, target in sides:
-            @pl.when(there)
-            def _():
-                x_copy(0, side, k, r, target).start()
+    for load in loads[:first]:
+        load.wait()
+    ice = ice_ref[...].astype(f32)
     for r in range(layers):
-        send_lat(0, r)
-    to_all(lambda q: grav_ref, g_in, g_send, g_recv)
-    to_all(lambda q: mat_ref, mat_in, t_send, t_recv)
+        pos = (rad * layers + (r + 1)).astype(f32) / total_rad
+        sbuf[r] = (load_scale * pos) * ice
+    for load in loads[first:]:
+        load.wait()
 
     quarter = nlon // 4
     block = layers * rows
@@ -417,8 +424,8 @@
         cols = slice(a * quarter, (a + 1) * quarter)
         return jnp.concatenate(
             [
-                u_ref[:, :, cols].reshape(block, quarter),
-                m_ref[:, :, cols].reshape(block, quarter),
+                ubuf[0, :, :, cols].reshape(block, quarter),
+                m_out[:, :, cols].reshape(block, quarter),
                 ice_ref[:, cols].astype(f32),
             ],
             axis=0,
@@ -436,6 +443,17 @@
         ],
         axis=1,
     )
+
+    pl.semaphore_wait(barrier, count - 1)
+    for k in range(CHUNKS):
+        for side, there, r, target in sides:
+            @pl.when(there)
+            def _():
+                x_copy(0, side, k, r, target).start()
+    for r in range(layers):
+        send_lat(0, r)
+    to_all(lambda q: grav_ref, g_in, g_send, g_recv)
+    to_all(lambda q: mat_ref, mat_in, t_send, t_recv)
 
     parts = []
     for h in range(halves):
@@ -482,7 +500,12 @@
     srow = lax.broadcasted_iota(jnp.int32, (degrees, LANES), 0)
     held = LANES // (layers * total_rad)
     cut = lane // (layers * total_rad) == lax.rem(srow, held)
-    repeat = repeat_ref[...]
+    lines = degrees // held
+    repeat = jnp.where(
+        lax.broadcasted_iota(jnp.int32, (degrees, lines), 0) // held
+        == lax.broadcasted_iota(jnp.int32, (degrees, lines), 1),
+        1.0, 0.0,
+    ).astype(jnp.bfloat16)
     wide = []
     for x in range(rad_n):
         lines = split(
@@ -495,9 +518,11 @@
     wide = split(jnp.concatenate(wide, axis=1))
     for d in range(total_rad):
         cols = slice(d * LANES, (d + 1) * LANES)
-        gexp[:, cols] = jnp.dot(
-            wide[0], expand_ref[:, cols], preferred_element_type=f32
-        ) + jnp.dot(wide[1], expand_ref[:, cols], preferred_element_type=f32)
+        at = (d // 2) * wide[0].shape[1]
+        place = expand_ref[at : at + wide[0].shape[1], (d % 2) * LANES : (d % 2 + 1) * LANES]
+        gexp[:, cols] = jnp.dot(wide[0], place, preferred_element_type=f32) + jnp.dot(
+            wide[1], place, preferred_element_type=f32
+        )
 
     jrow = lax.broadcasted_iota(jnp.int32, (rows, LANES), 0)
     jlane = (lax.broadcasted_iota(jnp.int32, (rows, LANES), 1) // layers) % rows
@@ -507,8 +532,13 @@
         for x in range(1, rad_n):
             line = line + mat_in[rad_n * i + x]
         ids.append(jnp.where(jrow == jlane, jnp.broadcast_to(line, (rows, LANES)), 0.0))
+    source_layer = lax.broadcasted_iota(jnp.int32, (LANES, LANES), 0)
+    source_layer = source_layer // block * layers + lax.rem(source_layer, layers)
+    spread = jnp.where(
+        source_layer == lax.broadcasted_iota(jnp.int32, (LANES, LANES), 1) // width, 1.0, 0.0
+    ).astype(jnp.bfloat16)
     ids = jnp.dot(
-        jnp.concatenate(ids, axis=0).astype(jnp.bfloat16), spread_ref[...],
+        jnp.concatenate(ids, axis=0).astype(jnp.bfloat16), spread,
         preferred_element_type=f32,
     )
     for n, table in enumerate((mu_ref, dec_ref, con_ref)):
@@ -633,6 +663,35 @@
     lax.fori_loop(0, last, drain, 0)
 
 
+def deliver_kernel(*refs):
+    count = (len(refs) - 1) // 2
+    sem = refs[-1]
+    copies = []
+    for n in range(count):
+        for r in range(refs[n].shape[0]):
+            copies.append(
+                pltpu.make_async_copy(refs[n].at[r], refs[count + n].at[:, r, :], sem.at[n, r])
+            )
+    for copy in copies:
+        copy.start()
+    for copy in copies:
+        copy.wait()
+
+
+def deliver(blocks):
+    layers, rows, nlon = blocks[0].shape
+    return tuple(
+        pl.pallas_call(
+            deliver_kernel,
+            out_shape=[jax.ShapeDtypeStruct((rows, layers, nlon), jnp.float32)] * len(blocks),
+            in_specs=[pl.BlockSpec(memory_space=pltpu.VMEM)] * len(blocks),
+            out_specs=[pl.BlockSpec(memory_space=pltpu.HBM)] * len(blocks),
+            scratch_shapes=[pltpu.SemaphoreType.DMA((len(blocks), layers))],
+            compiler_params=pltpu.CompilerParams(vmem_limit_bytes=4 << 20),
+        )(*blocks)
+    )
+
+
 def fused(displacement, memory, ice_class, stiff, decay, material, tables, gravity):
     lat_dev, r_dev, nlon = displacement.shape
     lat_n, rad_n = lax.axis_size("lat"), lax.axis_size("rad")
@@ -645,12 +704,6 @@
     fwd, inv = split_np(weighted), split_np(basis.T)
     orders = column_orders(MODES).reshape(count, width)
     shift = np.tile(2.0 * np.cos(2.0 * np.pi * orders / nlon), (1, total_rad)).astype(np.float32)
-    spread = np.zeros((LANES, LANES))
-    for x in range(rad_n):
-        for j in range(lat_dev):
-            for r in range(r_dev):
-                at = (x * r_dev + r) * width
-                spread[x * lat_dev * r_dev + j * r_dev + r, at : at + width] = 1.0
     held = LANES // (r_dev * total_rad)
     expand = np.zeros((rad_n, held, r_dev, total_rad, total_rad, total_rad, width))
     for x in range(rad_n):
@@ -658,30 +711,36 @@
             for d in range(total_rad):
                 to = x * r_dev + r
                 expand[x, :, r, (to - d) % total_rad, d, to, :] = 1.0
-    expand = expand.reshape(rad_n * LANES, total_rad * LANES)
-    repeat = np.repeat(np.eye(degrees // held), held, axis=0)
+    expand = expand.reshape(rad_n * LANES, total_rad // 2, 2 * LANES)
+    expand = expand.transpose(1, 0, 2).reshape(-1, 2 * LANES).astype(bf16)
+    tabs = [*even, *odd, expand, *fwd, *inv]
     rad = lax.axis_index("rad")
     ids = material.astype(f32).reshape(1, lat_dev * r_dev)
     ids = jnp.concatenate([jnp.where(rad == x, ids, 0.0) for x in range(rad_n)], axis=1)
     gravity = gravity.reshape(-1, LANES)
     lines = gravity.shape[0]
     operands = [
-        displacement.transpose(1, 0, 2), memory.transpose(1, 0, 2), ice_class, stiff, decay, ids, gravity,
-        *even, *odd, *fwd, *inv, shift,
-        spread.astype(bf16), expand.astype(bf16), repeat.astype(bf16), *tables,
+        displacement, memory, ice_class, np.concatenate(tabs, axis=0),
+        stiff, decay, ids, gravity, shift, *tables,
     ]
     operands = [jnp.asarray(x) for x in operands]
     vmem = pl.BlockSpec(memory_space=pltpu.VMEM)
     smem = pl.BlockSpec(memory_space=pltpu.SMEM)
+    hbm = pl.BlockSpec(memory_space=pltpu.HBM)
+    streamed = 4
     dma = pltpu.SemaphoreType.DMA
     steps = 2 * SWEEPS
     block = jax.ShapeDtypeStruct((r_dev, lat_dev, nlon), f32)
     out = pl.pallas_call(
         fused_kernel,
         out_shape=[block] * 3,
-        in_specs=[vmem] * (len(operands) - len(tables)) + [smem] * len(tables),
+        in_specs=[hbm] * streamed
+        + [vmem] * (len(operands) - streamed - len(tables))
+        + [smem] * len(tables),
         out_specs=[vmem] * 3,
-        scratch_shapes=[
+        scratch_shapes=[pltpu.VMEM(x.shape, x.dtype) for x in (ice_class, *tabs)]
+        + [
+            dma((2 * r_dev + 1 + len(tabs),)),
             pltpu.VMEM((steps + 1, r_dev, lat_dev, nlon), f32),
             pltpu.VMEM((r_dev, lat_dev, nlon), f32),
             pltpu.VMEM((steps, 2, lat_dev, nlon), f32),
@@ -700,12 +759,14 @@
             dma((steps, 2, CHUNKS)), dma((steps, 2, CHUNKS)),
             dma((steps, 2, r_dev)), dma((steps, 2, r_dev)),
         ] + [dma((count,))] * 10,
-        compiler_params=pltpu.CompilerParams(collective_id=2, has_side_effects=True),
+        compiler_params=pltpu.CompilerParams(
+            collective_id=2, has_side_effects=True, vmem_limit_bytes=54500000
+        ),
     )(*operands)
-    return tuple(x.transpose(1, 0, 2) for x in out)
-
-
-def fits(lat_dev, r_dev, total_rad, rad_n, count):
+    return deliver(out)
+
+
+def fits(lat_dev, r_dev, total_lat, total_rad, rad_n, count, degrees):
     width = 2 * MODES // count
     return (
         rad_n == 2
@@ -714,6 +775,9 @@
         and width * total_rad == LANES
         and rad_n * lat_dev * r_dev == LANES
         and LANES % (r_dev * total_rad) == 0
+        and total_rad % 2 == 0
+        and degrees == 2 * LANES
+        and total_lat == 2 * LANES
     )
 
 
@@ -736,7 +800,8 @@
         jnp.float32
     ) / total_rad
     source = load_scale * ice_class.astype(jnp.float32)[None, :, :] * layer_pos[:, None, None]
-    if fits(lat_dev, r_dev, total_rad, rad_count, lat_count * rad_count):
+    devices = lat_count * rad_count
+    if fits(lat_dev, r_dev, total_lat, total_rad, rad_count, devices, degrees):
         tables = (mu_table, decay_table, contrast_table)
         return fused(
             displacement, memory, ice_class, stiff, decay, material, tables, gravity_kernel

time: 59.6 us -> 54.2 us (0.909)
  local copies, waits for them, and re-layouts: 11.2 us -> 5.03 us
  other arithmetic: 0.71 us -> 1.54 us
    transpose x1 -> x0, local copies, waits for them, and re-layouts: 2.77 us -> none  [fused(): memory.transpose(1, 0, 2)]
    unnamed x16 -> x11, local copies, waits for them, and re-layouts: 5.93 us -> 4.38 us
    reduce_sum x1, other arithmetic: 0.09 us -> 0.77 us  [lookup(): return jnp.sum(onehot * table[None, None, :], axis=-1)]
    select_n x1, other arithmetic: 0.01 us -> 0.69 us  [fused(): jnp.where(rad == x, ids, 0.0)]
    broadcast_in_dim x1, local copies, waits for them, and re-layouts: 0.71 us -> 0.1 us  [per_device(): decay = lookup(material.T, decay_table)[:, :, None]]
    broadcast_in_dim x1, local copies, waits for them, and re-layouts: 0.71 us -> 0.1 us  [per_device(): stiff = lookup(material.T, mu_table)[:, :, None]]
    pallas_call x1 -> x2, Pallas kernels: 46.5 us -> 46.6 us  [the longest x1 45.4 us: fused(): pl.pallas_call(fused_kernel, out_shape=[block] * 3, in_specs=[hbm] * stre...]
where the time goes in v1:
time: 54.2 us; the launch traced here: 53.8 us
  Pallas kernels  46.6 us (86%)
  local copies, waits for them, and re-layouts  5.03 us (9%)
  other arithmetic  1.54 us (3%)
  between operations  0.67 us (1%)
    pallas_call x1, Pallas kernels, fused(): pl.pallas_call(fused_kernel, out_shape=[block] * 3, in_specs=[hbm] * stre...  45.4 us
    unnamed x11, local copies, waits for them, and re-layouts  4.38 us
    pallas_call x1, Pallas kernels, deliver(): pl.pallas_call(deliver_kernel, out_shape=[jax.ShapeDtypeStruct((rows, lay...  1.24 us

profile of v1, /device:TPU:0, one launch (start us, length us, event | category | flops | bytes accessed | tf_op | source)
XLA Modules:
  0.0 53.8 jit_solution(18086113053321805589)
XLA Ops:
  0.6 0.7 %convert_select_fusion.1 = (f32[16,4]{0,1:T(4,128)S(1)}, f32[16,4]{0,1:T(4,128)S(1)}) fusion(s32[16,4]{0,1:T(4,128)} %param.13, pred[]{:T(512)S(6)} %eq.13, pred[]{:T(512)S(6)} %eq.14), kind=kLoop, calls=%fused_computation.4 | loop fusion | flops 192 | bytes 770 | tf_op jit(solution)/shard_map/jit(_where)/select_n | solution.py:719
  1.3 0.8 %select_reduce_fusion = (f32[4,16]{1,0:T(4,128)S(1)}, f32[4,16]{1,0:T(4,128)S(1)}) fusion(f32[8]{0:T(128)} %dec_ref.1, s32[4,16]{1,0:T(4,128)} %bitcast.3, f32[8]{0:T(128)} %mu_ref.1), kind=kLoop, calls=%fused_computation | loop fusion | flops 2432 | bytes 832 | tf_op jit(solution)/shard_map/reduce_sum | solution.py:23
  2.1 0.1 copy.23
  2.2 0.1 select_n.38
  2.3 0.1 copy.24
  2.4 0.1 select_n.41
  2.4 0.1 pad_maximum_fusion.mat_ref
  2.5 0.1 copy.26.stiff_ref
  2.6 0.1 copy.27.decay_ref
  2.7 0.8 %copy.25 = f32[16,4,8]{2,1,0:T(4,128)S(1)} copy(f32[16,4,8]{0,2,1:T(8,128)} %param.17) | data formatting | bytes 4096 | tf_op args[7]
  3.5 0.1 reshape.43.grav_ref
  3.6 0.0 copy-start
  3.6 0.9 %copy-done = s32[16,2048]{1,0:T(8,128)S(1)} copy-done((s32[16,2048]{1,0:T(8,128)S(1)}, s32[16,2048]{1,0:T(8,128)}, u32[]{:S(2)}) %copy-start) | copy-done | bytes 131096
  4.5 0.0 copy-start.1
  4.5 0.7 %copy-done.1 = f32[32,128]{1,0:T(8,128)S(1)} copy-done((f32[32,128]{1,0:T(8,128)S(1)}, f32[32,128]{1,0:T(8,128)}, u32[]{:S(2)}) %copy-start.1) | copy-done | bytes 16408
  5.3 0.0 copy-start.2
  5.3 0.7 %copy-done.2 = f32[8]{0:T(128)S(1)} copy-done((f32[8]{0:T(128)S(1)}, f32[8]{0:T(128)}, u32[]{:S(2)}) %copy-start.2) | copy-done | bytes 56
  5.9 0.0 copy-start.3
  5.9 0.7 %copy-done.3 = f32[8]{0:T(128)S(1)} copy-done((f32[8]{0:T(128)S(1)}, f32[8]{0:T(128)}, u32[]{:S(2)}) %copy-start.3) | copy-done | bytes 56
  6.6 0.0 copy-start.4
  6.6 0.7 %copy-done.4 = f32[8]{0:T(128)S(1)} copy-done((f32[8]{0:T(128)S(1)}, f32[8]{0:T(128)}, u32[]{:S(2)}) %copy-start.4) | copy-done | bytes 56
  7.2 45.4 %shard_map.121 = (f32[4,16,2048]{2,1,0:T(8,128)S(1)}, f32[4,16,2048]{2,1,0:T(8,128)S(1)}, f32[4,16,2048]{2,1,0:T(8,128)S(1)}) custom-call(f32[16,4,2048]{2,1,0:T(4,128)} %u_ref.1, f32[16,4,2048]{2,1,0:T(4,128)} %m_ref.1, s32[16,2048]{1,0:T(8,128)S(1)} %copy-done, bf16[5120,256]{1,0:T(8,128)(2,1)} %constant.16.clone.table_hbm, ...), custom_call_target="tpu_custom_call" | custom-call | tf_op jit(solution)/shard_map/pallas_call | solution.py:734
  52.6 1.2 %shard_map.122 = (f32[16,4,2048]{2,1,0:T(4,128)}, f32[16,4,2048]{2,1,0:T(4,128)}, f32[16,4,2048]{2,1,0:T(4,128)}) custom-call(f32[4,16,2048]{2,1,0:T(8,128)S(1)} %get-tuple-element.6.refs_0_, f32[4,16,2048]{2,1,0:T(8,128)S(1)} %get-tuple-element.7.refs_1_, f32[4,16,2048]{2,1,0:T(8,128)S(1)} %get-tuple-element.8.refs_2_), custom_call_target="tpu_custom_call" | custom-call | tf_op jit(solution)/shard_map/pallas_call | solution.py:684
Async XLA Ops:
  3.6 0.9 %copy-start = (s32[16,2048]{1,0:T(8,128)S(1)}, s32[16,2048]{1,0:T(8,128)}, u32[]{:S(2)}) copy-start(s32[16,2048]{1,0:T(8,128)} %ice_hbm.1) | copy-start | bytes 393220
  4.5 0.7 %copy-start.1 = (f32[32,128]{1,0:T(8,128)S(1)}, f32[32,128]{1,0:T(8,128)}, u32[]{:S(2)}) copy-start(f32[32,128]{1,0:T(8,128)} %constant.17.clone.shift_ref) | copy-start | bytes 49156
  5.3 0.7 %copy-start.2 = (f32[8]{0:T(128)S(1)}, f32[8]{0:T(128)}, u32[]{:S(2)}) copy-start(f32[8]{0:T(128)} %dec_ref.1) | copy-start | bytes 100
  5.9 0.7 %copy-start.3 = (f32[8]{0:T(128)S(1)}, f32[8]{0:T(128)}, u32[]{:S(2)}) copy-start(f32[8]{0:T(128)} %mu_ref.1) | copy-start | bytes 100
  6.6 0.7 %copy-start.4 = (f32[8]{0:T(128)S(1)}, f32[8]{0:T(128)}, u32[]{:S(2)}) copy-start(f32[8]{0:T(128)} %con_ref.1) | copy-start | bytes 100

commit v2 on v1

--- a/solution.py
+++ b/solution.py
@@ -240,10 +240,11 @@
 
 
 def fused_kernel(
-    u_ref, m_ref, ice_hbm, table_hbm, stiff_ref, decay_ref, mat_ref, grav_ref,
-    shift_ref, mu_ref, dec_ref, con_ref,
+    u_ref, m_ref, ice_hbm, material_hbm, gravity_hbm, mu_hbm, dec_hbm, con_hbm, shift_hbm, table_hbm,
     u_out, m_out, p_out,
-    ice_ref, even_hi, even_lo, odd_hi, odd_lo, expand_ref, fwd_hi, fwd_lo, inv_hi, inv_lo, load_sem,
+    ice_ref, material, gravity, mu_ref, dec_ref, con_ref, shift_ref, pad,
+    stiff_ref, decay_ref, mat_ref, grav_ref,
+    even_hi, even_lo, odd_hi, odd_lo, fwd_hi, fwd_lo, inv_hi, inv_lo, load_sem,
     ubuf, sbuf, x_in, lat_out, lat_in, g_in, mat_in, pack_out, pack_in, ice_out, ice_in,
     back_out, back_in, gexp, par,
     x_send, x_recv, l_send, l_recv, g_send, g_recv, t_send, t_recv,
@@ -282,15 +283,18 @@
 
     pairs = [(u_ref.at[:, r, :], ubuf.at[0, r]) for r in range(layers)]
     pairs += [(m_ref.at[:, r, :], m_out.at[r]) for r in range(layers)]
-    pairs.append((ice_hbm, ice_ref))
+    pairs += [
+        (ice_hbm, ice_ref), (material_hbm, material), (gravity_hbm, gravity), (mu_hbm, mu_ref),
+        (dec_hbm, dec_ref), (con_hbm, con_ref), (shift_hbm, shift_ref),
+    ]
+    first = len(pairs)
     at = 0
-    for held in (even_hi, even_lo, odd_hi, odd_lo, expand_ref, fwd_hi, fwd_lo, inv_hi, inv_lo):
+    for held in (even_hi, even_lo, odd_hi, odd_lo, fwd_hi, fwd_lo, inv_hi, inv_lo):
         pairs.append((table_hbm.at[pl.ds(at, held.shape[0])], held))
         at += held.shape[0]
     loads = [pltpu.make_async_copy(a, b, load_sem.at[n]) for n, (a, b) in enumerate(pairs)]
     for load in loads:
         load.start()
-    first = 2 * layers + 1
 
     def remote(src, dst, send_sem, recv_sem, target):
         return pltpu.make_async_remote_copy(
@@ -406,10 +410,39 @@
         def _():
             for s in range(last):
                 lat_in[s, side] = jnp.zeros(lat_in.shape[2:], f32)
+    for load in loads[:first]:
+        load.wait()
+    pad[...] = jnp.zeros_like(pad)
+    pad[0, :layers, :rows] = material[...].astype(f32)
+    own = gravity.shape[2]
+    for r in range(layers):
+        pad[1 + r, :, :own] = gravity[r]
+    prow = lax.broadcasted_iota(jnp.int32, (rows, LANES), 0)
+    plane = lax.broadcasted_iota(jnp.int32, (rows, LANES), 1)
+    line = jnp.zeros((1, LANES), f32)
+    for r in range(layers):
+        kind = pad[0, r : r + 1]
+        for x in range(rad_n):
+            at = (x * layers + r) * rows
+            line += jnp.where(rad == x, pltpu.roll(kind, at, 1) if at else kind, 0.0)
+        column = jnp.sum(jnp.where(prow == plane, kind, 0.0), axis=1, keepdims=True)
+        for table, held in ((mu_ref, stiff_ref), (dec_ref, decay_ref)):
+            value = jnp.zeros((rows, 1), f32)
+            for k in range(table.shape[0]):
+                value = jnp.where(column == k, table[k], value)
+            held[r] = value
+        full = pad[1 + r]
+        step = own
+        while step < LANES:
+            full = full + pltpu.roll(full, step, 1)
+            step *= 2
+        keep = lax.broadcasted_iota(jnp.int32, full.shape, 1) // own == lax.broadcasted_iota(
+            jnp.int32, full.shape, 0
+        )
+        grav_ref[r : r + 1] = jnp.sum(jnp.where(keep, full, 0.0), axis=0, keepdims=True)
+    mat_ref[...] = line
     g_in[me] = grav_ref[...]
     mat_in[me] = mat_ref[...]
-    for load in loads[:first]:
-        load.wait()
     ice = ice_ref[...].astype(f32)
     for r in range(layers):
         pos = (rad * layers + (r + 1)).astype(f32) / total_rad
@@ -496,36 +529,47 @@
     each(lambda q: grav_ref, g_in, g_send, g_recv, "recv")
     each(lambda q: mat_ref, mat_in, t_send, t_recv, "recv")
     degrees = fwd_hi.shape[0]
-    lane = lax.broadcasted_iota(jnp.int32, (degrees, LANES), 1)
-    srow = lax.broadcasted_iota(jnp.int32, (degrees, LANES), 0)
-    held = LANES // (layers * total_rad)
-    cut = lane // (layers * total_rad) == lax.rem(srow, held)
-    lines = degrees // held
-    repeat = jnp.where(
-        lax.broadcasted_iota(jnp.int32, (degrees, lines), 0) // held
-        == lax.broadcasted_iota(jnp.int32, (degrees, lines), 1),
+    own = degrees // lat_n
+    cut = lax.rem(lax.broadcasted_iota(jnp.int32, (own, LANES), 1), own) == (
+        lax.broadcasted_iota(jnp.int32, (own, LANES), 0)
+    )
+    wide = []
+    for x in range(rad_n):
+        for r in range(layers):
+            wide.append(
+                jnp.concatenate(
+                    [
+                        jnp.where(
+                            cut, jnp.broadcast_to(g_in[rad_n * i + x, r : r + 1], (own, LANES)), 0.0
+                        )
+                        for i in range(lat_n)
+                    ],
+                    axis=0,
+                )
+            )
+    wide = split(jnp.concatenate(wide, axis=1))
+    entries = total_rad * total_rad
+    gather = jnp.where(
+        lax.broadcasted_iota(jnp.int32, (wide[0].shape[1], entries), 0) // own
+        == lax.broadcasted_iota(jnp.int32, (wide[0].shape[1], entries), 1),
         1.0, 0.0,
     ).astype(jnp.bfloat16)
-    wide = []
-    for x in range(rad_n):
-        lines = split(
-            jnp.concatenate([g_in[rad_n * i + x] for i in range(lat_n)], axis=0)
-        )
-        full = jnp.dot(repeat, lines[0], preferred_element_type=f32) + jnp.dot(
-            repeat, lines[1], preferred_element_type=f32
-        )
-        wide.append(jnp.where(cut, full, 0.0))
-    wide = split(jnp.concatenate(wide, axis=1))
+    wide = split(
+        jnp.dot(wide[0], gather, preferred_element_type=f32)
+        + jnp.dot(wide[1], gather, preferred_element_type=f32)
+    )
+    entry = lax.broadcasted_iota(jnp.int32, (entries, LANES), 0)
+    target = lax.broadcasted_iota(jnp.int32, (entries, LANES), 1) // width
     for d in range(total_rad):
         cols = slice(d * LANES, (d + 1) * LANES)
-        at = (d // 2) * wide[0].shape[1]
-        place = expand_ref[at : at + wide[0].shape[1], (d % 2) * LANES : (d % 2 + 1) * LANES]
+        origin = lax.rem(target + (total_rad - d), total_rad)
+        place = jnp.where(entry == target * total_rad + origin, 1.0, 0.0).astype(jnp.bfloat16)
         gexp[:, cols] = jnp.dot(wide[0], place, preferred_element_type=f32) + jnp.dot(
             wide[1], place, preferred_element_type=f32
         )
 
     jrow = lax.broadcasted_iota(jnp.int32, (rows, LANES), 0)
-    jlane = (lax.broadcasted_iota(jnp.int32, (rows, LANES), 1) // layers) % rows
+    jlane = (lax.broadcasted_iota(jnp.int32, (rows, LANES), 1)) % rows
     ids = []
     for i in range(lat_n):
         line = mat_in[rad_n * i]
@@ -533,7 +577,7 @@
             line = line + mat_in[rad_n * i + x]
         ids.append(jnp.where(jrow == jlane, jnp.broadcast_to(line, (rows, LANES)), 0.0))
     source_layer = lax.broadcasted_iota(jnp.int32, (LANES, LANES), 0)
-    source_layer = source_layer // block * layers + lax.rem(source_layer, layers)
+    source_layer = source_layer // rows
     spread = jnp.where(
         source_layer == lax.broadcasted_iota(jnp.int32, (LANES, LANES), 1) // width, 1.0, 0.0
     ).astype(jnp.bfloat16)
@@ -692,7 +736,7 @@
     )
 
 
-def fused(displacement, memory, ice_class, stiff, decay, material, tables, gravity):
+def fused(displacement, memory, ice_class, material, tables, gravity):
     lat_dev, r_dev, nlon = displacement.shape
     lat_n, rad_n = lax.axis_size("lat"), lax.axis_size("rad")
     count, total_lat, total_rad = lat_n * rad_n, lat_n * lat_dev, rad_n * r_dev
@@ -704,49 +748,41 @@
     fwd, inv = split_np(weighted), split_np(basis.T)
     orders = column_orders(MODES).reshape(count, width)
     shift = np.tile(2.0 * np.cos(2.0 * np.pi * orders / nlon), (1, total_rad)).astype(np.float32)
-    held = LANES // (r_dev * total_rad)
-    expand = np.zeros((rad_n, held, r_dev, total_rad, total_rad, total_rad, width))
-    for x in range(rad_n):
-        for r in range(r_dev):
-            for d in range(total_rad):
-                to = x * r_dev + r
-                expand[x, :, r, (to - d) % total_rad, d, to, :] = 1.0
-    expand = expand.reshape(rad_n * LANES, total_rad // 2, 2 * LANES)
-    expand = expand.transpose(1, 0, 2).reshape(-1, 2 * LANES).astype(bf16)
-    tabs = [*even, *odd, expand, *fwd, *inv]
-    rad = lax.axis_index("rad")
-    ids = material.astype(f32).reshape(1, lat_dev * r_dev)
-    ids = jnp.concatenate([jnp.where(rad == x, ids, 0.0) for x in range(rad_n)], axis=1)
-    gravity = gravity.reshape(-1, LANES)
-    lines = gravity.shape[0]
+    tabs = [*even, *odd, *fwd, *inv]
+    gravity = gravity.transpose(1, 2, 0)
     operands = [
-        displacement, memory, ice_class, np.concatenate(tabs, axis=0),
-        stiff, decay, ids, gravity, shift, *tables,
+        displacement, memory, ice_class, material.T, gravity, *tables, shift, np.concatenate(tabs, axis=0)
     ]
-    operands = [jnp.asarray(x) for x in operands]
+    operands = [pltpu.with_memory_space_constraint(jnp.asarray(x), pltpu.HBM) for x in operands]
     vmem = pl.BlockSpec(memory_space=pltpu.VMEM)
-    smem = pl.BlockSpec(memory_space=pltpu.SMEM)
     hbm = pl.BlockSpec(memory_space=pltpu.HBM)
-    streamed = 4
     dma = pltpu.SemaphoreType.DMA
     steps = 2 * SWEEPS
     block = jax.ShapeDtypeStruct((r_dev, lat_dev, nlon), f32)
     out = pl.pallas_call(
         fused_kernel,
         out_shape=[block] * 3,
-        in_specs=[hbm] * streamed
-        + [vmem] * (len(operands) - streamed - len(tables))
-        + [smem] * len(tables),
+        in_specs=[hbm] * len(operands),
         out_specs=[vmem] * 3,
-        scratch_shapes=[pltpu.VMEM(x.shape, x.dtype) for x in (ice_class, *tabs)]
+        scratch_shapes=[pltpu.VMEM(x.shape, x.dtype) for x in operands[2:5]]
+        + [pltpu.SMEM(x.shape, x.dtype) for x in tables]
         + [
-            dma((2 * r_dev + 1 + len(tabs),)),
+            pltpu.VMEM(shift.shape, f32),
+            pltpu.VMEM((1 + r_dev, 8, LANES), f32),
+            pltpu.VMEM((r_dev, lat_dev, 1), f32),
+            pltpu.VMEM((r_dev, lat_dev, 1), f32),
+            pltpu.VMEM((1, LANES), f32),
+            pltpu.VMEM((r_dev, LANES), f32),
+        ]
+        + [pltpu.VMEM(x.shape, x.dtype) for x in tabs]
+        + [
+            dma((2 * r_dev + 7 + len(tabs),)),
             pltpu.VMEM((steps + 1, r_dev, lat_dev, nlon), f32),
             pltpu.VMEM((r_dev, lat_dev, nlon), f32),
             pltpu.VMEM((steps, 2, lat_dev, nlon), f32),
             pltpu.VMEM((steps, 2, r_dev, 1, nlon), f32),
             pltpu.VMEM((steps, 2, r_dev, 1, nlon), f32),
-            pltpu.VMEM((count, lines, LANES), f32),
+            pltpu.VMEM((count, r_dev, LANES), f32),
             pltpu.VMEM((count, 1, LANES), f32),
             pltpu.VMEM((count, 16, LANES), f32),
             pltpu.VMEM((count, 16, LANES), f32),
@@ -760,7 +796,7 @@
             dma((steps, 2, r_dev)), dma((steps, 2, r_dev)),
         ] + [dma((count,))] * 10,
         compiler_params=pltpu.CompilerParams(
-            collective_id=2, has_side_effects=True, vmem_limit_bytes=54500000
+            collective_id=2, has_side_effects=True, vmem_limit_bytes=40 << 20
         ),
     )(*operands)
     return deliver(out)
@@ -774,8 +810,9 @@
         and width * count == 2 * MODES
         and width * total_rad == LANES
         and rad_n * lat_dev * r_dev == LANES
-        and LANES % (r_dev * total_rad) == 0
-        and total_rad % 2 == 0
+        and total_rad * (degrees * rad_n // count) == LANES
+        and total_rad % 8 == 0
+        and r_dev <= 8
         and degrees == 2 * LANES
         and total_lat == 2 * LANES
     )
@@ -804,7 +841,7 @@
     if fits(lat_dev, r_dev, total_lat, total_rad, rad_count, devices, degrees):
         tables = (mu_table, decay_table, contrast_table)
         return fused(
-            displacement, memory, ice_class, stiff, decay, material, tables, gravity_kernel
+            displacement, memory, ice_class, material, tables, gravity_kernel
         )
     basis, weighted = legendre(total_lat, degrees)
     projection = jnp.asarray(

time: 54.2 us -> 46.9 us (0.87)
  local copies, waits for them, and re-layouts: 5.03 us -> 0 us
  other arithmetic: 1.54 us -> 0 us
    unnamed x11 -> x0, local copies, waits for them, and re-layouts: 4.38 us -> none
    reduce_sum x1 -> x0, other arithmetic: 0.77 us -> none  [lookup(): return jnp.sum(onehot * table[None, None, :], axis=-1)]
    select_n x1 -> x0, other arithmetic: 0.69 us -> none  [fused(): jnp.where(rad == x, ids, 0.0)]
where the time goes in v2:
time: 46.9 us; the launch traced here: 46.8 us
  Pallas kernels  46.1 us (98%)
  between operations  0.64 us (1%)
    pallas_call x1, Pallas kernels, fused(): pl.pallas_call(fused_kernel, out_shape=[block] * 3, in_specs=[hbm] * len(...  44.9 us
    pallas_call x1, Pallas kernels, deliver(): pl.pallas_call(deliver_kernel, out_shape=[jax.ShapeDtypeStruct((rows, lay...  1.24 us

profile of v2, /device:TPU:0, one launch (start us, length us, event | category | flops | bytes accessed | tf_op | source)
XLA Modules:
  0.0 46.8 jit_solution(5118923367024790702)
XLA Ops:
  0.6 44.9 %shard_map.121 = (f32[4,16,2048]{2,1,0:T(8,128)S(1)}, f32[4,16,2048]{2,1,0:T(8,128)S(1)}, f32[4,16,2048]{2,1,0:T(8,128)S(1)}) custom-call(f32[16,4,2048]{2,1,0:T(4,128)} %u_ref.1, f32[16,4,2048]{2,1,0:T(4,128)} %m_ref.1, s32[16,2048]{1,0:T(8,128)} %ice_hbm.1, s32[4,16]{1,0:T(4,128)} %bitcast.3, f32[4,8,16]{2,1,0:T(8,128)} %bitcast.2, f32[8]{0:T(128)} %mu_hbm.1, ...), custom_call_target="tpu_custom_call" | custom-call | tf_op jit(solution)/shard_map/pallas_call | solution.py:762
  45.5 1.2 %shard_map.122 = (f32[16,4,2048]{2,1,0:T(4,128)}, f32[16,4,2048]{2,1,0:T(4,128)}, f32[16,4,2048]{2,1,0:T(4,128)}) custom-call(f32[4,16,2048]{2,1,0:T(8,128)S(1)} %get-tuple-element.6.refs_0_, f32[4,16,2048]{2,1,0:T(8,128)S(1)} %get-tuple-element.7.refs_1_, f32[4,16,2048]{2,1,0:T(8,128)S(1)} %get-tuple-element.8.refs_2_), custom_call_target="tpu_custom_call" | custom-call | tf_op jit(solution)/shard_map/pallas_call | solution.py:728

commit v3 on v2

--- a/solution.py
+++ b/solution.py
@@ -243,12 +243,11 @@
     u_ref, m_ref, ice_hbm, material_hbm, gravity_hbm, mu_hbm, dec_hbm, con_hbm, shift_hbm, table_hbm,
     u_out, m_out, p_out,
     ice_ref, material, gravity, mu_ref, dec_ref, con_ref, shift_ref, pad,
-    stiff_ref, decay_ref, mat_ref, grav_ref,
+    stiff_ref, decay_ref, grav_ref,
     even_hi, even_lo, odd_hi, odd_lo, fwd_hi, fwd_lo, inv_hi, inv_lo, load_sem,
-    ubuf, sbuf, x_in, lat_out, lat_in, g_in, mat_in, pack_out, pack_in, ice_out, ice_in,
+    ubuf, sbuf, x_in, lat_out, lat_in, g_in, pack_out, pack_in,
     back_out, back_in, gexp, par,
-    x_send, x_recv, l_send, l_recv, g_send, g_recv, t_send, t_recv,
-    a_send, a_recv, i_send, i_recv, b_send, b_recv,
+    x_send, x_recv, l_send, l_recv, g_send, g_recv, a_send, a_recv, b_send, b_recv,
 ):
     f32 = jnp.float32
     rows, layers, nlon = u_ref.shape
@@ -304,6 +303,8 @@
 
     def to_all(src_of, dst, send_sem, recv_sem):
         def start(d, carry):
+            far = d // 2
+            d = count // 2 + jnp.where(lax.rem(d, 2) == 1, far, -far)
             q = peer(d)
             remote(src_of(q), dst.at[me], send_sem.at[d], recv_sem.at[d], device(q)).start()
             return carry
@@ -440,9 +441,8 @@
             jnp.int32, full.shape, 0
         )
         grav_ref[r : r + 1] = jnp.sum(jnp.where(keep, full, 0.0), axis=0, keepdims=True)
-    mat_ref[...] = line
+    grav_ref[layers : layers + 1] = line
     g_in[me] = grav_ref[...]
-    mat_in[me] = mat_ref[...]
     ice = ice_ref[...].astype(f32)
     for r in range(layers):
         pos = (rad * layers + (r + 1)).astype(f32) / total_rad
@@ -486,7 +486,6 @@
     for r in range(layers):
         send_lat(0, r)
     to_all(lambda q: grav_ref, g_in, g_send, g_recv)
-    to_all(lambda q: mat_ref, mat_in, t_send, t_recv)
 
     parts = []
     for h in range(halves):
@@ -504,9 +503,7 @@
             )
     for p, part in enumerate(swap_groups(parts, width)):
         for t in range(tiles):
-            pack_out[per_tile * t + p] = part[16 * t : 16 * (t + 1)]
-    to_all(lambda q: pack_out.at[q], pack_in, a_send, a_recv)
-    pack_in[me] = pack_out[me]
+            pack_out[per_tile * t + p, 0:16] = part[16 * t : 16 * (t + 1)]
 
     sub8 = lax.broadcasted_iota(jnp.int32, (8, LANES), 0)
     group8 = lax.broadcasted_iota(jnp.int32, (8, LANES), 1) // width
@@ -522,12 +519,11 @@
             down = pltpu.roll(pltpu.roll(x, step, 0), LANES - width * step, 1)
             x = jnp.where(sb == gb, x, jnp.where(gb == 1, up, down))
         for p in range(per_tile):
-            ice_out[per_tile * t + p] = x[p : p + 1]
-    to_all(lambda q: ice_out.at[q], ice_in, i_send, i_recv)
-    ice_in[me] = ice_out[me]
+            pack_out[per_tile * t + p, 16:17] = x[p : p + 1]
+    to_all(lambda q: pack_out.at[q], pack_in, a_send, a_recv)
+    pack_in[me] = pack_out[me]
 
     each(lambda q: grav_ref, g_in, g_send, g_recv, "recv")
-    each(lambda q: mat_ref, mat_in, t_send, t_recv, "recv")
     degrees = fwd_hi.shape[0]
     own = degrees // lat_n
     cut = lax.rem(lax.broadcasted_iota(jnp.int32, (own, LANES), 1), own) == (
@@ -572,9 +568,9 @@
     jlane = (lax.broadcasted_iota(jnp.int32, (rows, LANES), 1)) % rows
     ids = []
     for i in range(lat_n):
-        line = mat_in[rad_n * i]
+        line = g_in[rad_n * i, layers : layers + 1]
         for x in range(1, rad_n):
-            line = line + mat_in[rad_n * i + x]
+            line = line + g_in[rad_n * i + x, layers : layers + 1]
         ids.append(jnp.where(jrow == jlane, jnp.broadcast_to(line, (rows, LANES)), 0.0))
     source_layer = lax.broadcasted_iota(jnp.int32, (LANES, LANES), 0)
     source_layer = source_layer // rows
@@ -595,22 +591,25 @@
         sweep(s, True)
         return carry
 
-    lax.fori_loop(0, SWEEPS - 1, two, 0)
+    lax.fori_loop(0, 1, two, 0)
 
     each(lambda q: pack_out.at[q], pack_in, a_send, a_recv, "recv")
-    each(lambda q: ice_out.at[q], ice_in, i_send, i_recv, "recv")
     near = lax.broadcasted_iota(jnp.int32, (16, LANES), 1) < LANES // 2
     us, qs, ss = [], [], []
     sub = lax.broadcasted_iota(jnp.int32, (8, LANES), 0)
     for i in range(lat_n):
-        a, b = pack_in[rad_n * i], pack_in[rad_n * i + 1]
+        a, b = pack_in[rad_n * i, 0:16], pack_in[rad_n * i + 1, 0:16]
         top = jnp.where(near, a, pltpu.roll(b, LANES // 2, 1))
         low = jnp.where(near, pltpu.roll(a, LANES // 2, 1), b)
         us += [top[:8], low[:8]]
         qs += [top[8:], low[8:]]
         for x in range(rad_n):
             ss.append(
-                jnp.where(sub == group8, jnp.broadcast_to(ice_in[rad_n * i + x], (8, LANES)), 0.0)
+                jnp.where(
+                    sub == group8,
+                    jnp.broadcast_to(pack_in[rad_n * i + x, 16:17], (8, LANES)),
+                    0.0,
+                )
             )
     u, q, s_hat = (jnp.concatenate(v, axis=0) for v in (us, qs, ss))
     step = width
@@ -649,7 +648,7 @@
     to_all(lambda q: back_out.at[q], back_in, b_send, b_recv)
     back_in[me] = back_out[me]
 
-    sweep(SWEEPS - 1, True)
+    lax.fori_loop(1, SWEEPS, two, 0)
 
     each(lambda q: back_out.at[q], back_in, b_send, b_recv, "recv")
     parts = swap_groups(
@@ -686,9 +685,7 @@
     u_out[...] = ubuf[last]
 
     each(lambda q: grav_ref, g_in, g_send, g_recv, "send")
-    each(lambda q: mat_ref, mat_in, t_send, t_recv, "send")
     each(lambda q: pack_out.at[q], pack_in, a_send, a_recv, "send")
-    each(lambda q: ice_out.at[q], ice_in, i_send, i_recv, "send")
     each(lambda q: back_out.at[q], back_in, b_send, b_recv, "send")
 
     def drain(s, carry):
@@ -771,8 +768,7 @@
             pltpu.VMEM((1 + r_dev, 8, LANES), f32),
             pltpu.VMEM((r_dev, lat_dev, 1), f32),
             pltpu.VMEM((r_dev, lat_dev, 1), f32),
-            pltpu.VMEM((1, LANES), f32),
-            pltpu.VMEM((r_dev, LANES), f32),
+            pltpu.VMEM((r_dev + 1, LANES), f32),
         ]
         + [pltpu.VMEM(x.shape, x.dtype) for x in tabs]
         + [
@@ -782,19 +778,16 @@
             pltpu.VMEM((steps, 2, lat_dev, nlon), f32),
             pltpu.VMEM((steps, 2, r_dev, 1, nlon), f32),
             pltpu.VMEM((steps, 2, r_dev, 1, nlon), f32),
-            pltpu.VMEM((count, r_dev, LANES), f32),
-            pltpu.VMEM((count, 1, LANES), f32),
-            pltpu.VMEM((count, 16, LANES), f32),
-            pltpu.VMEM((count, 16, LANES), f32),
-            pltpu.VMEM((count, 1, LANES), f32),
-            pltpu.VMEM((count, 1, LANES), f32),
+            pltpu.VMEM((count, r_dev + 1, LANES), f32),
+            pltpu.VMEM((count, 17, LANES), f32),
+            pltpu.VMEM((count, 17, LANES), f32),
             pltpu.VMEM((count, 8, LANES), f32),
             pltpu.VMEM((count, 8, LANES), f32),
             pltpu.VMEM((degrees, total_rad * LANES), f32),
             pltpu.VMEM((3, total_lat, LANES), f32),
             dma((steps, 2, CHUNKS)), dma((steps, 2, CHUNKS)),
             dma((steps, 2, r_dev)), dma((steps, 2, r_dev)),
-        ] + [dma((count,))] * 10,
+        ] + [dma((count,))] * 6,
         compiler_params=pltpu.CompilerParams(
             collective_id=2, has_side_effects=True, vmem_limit_bytes=40 << 20
         ),

time: 46.9 us -> 43 us (0.917)
  Pallas kernels: 46.1 us -> 41.8 us
    pallas_call x1, Pallas kernels: 44.9 us -> 40.6 us  [fused(): pl.pallas_call(fused_kernel, out_shape=[block] * 3, in_specs=[hbm] * len(...]
where the time goes in v3:
time: 43 us; the launch traced here: 42.4 us
  Pallas kernels  41.8 us (97%)
  between operations  0.64 us (1%)
    pallas_call x1, Pallas kernels, fused(): pl.pallas_call(fused_kernel, out_shape=[block] * 3, in_specs=[hbm] * len(...  40.6 us
    pallas_call x1, Pallas kernels, deliver(): pl.pallas_call(deliver_kernel, out_shape=[jax.ShapeDtypeStruct((rows, lay...  1.24 us

profile of v3, /device:TPU:0, one launch (start us, length us, event | category | flops | bytes accessed | tf_op | source)
XLA Modules:
  0.0 42.4 jit_solution(4894701750248594025)
XLA Ops:
  0.6 40.6 %shard_map.121 = (f32[4,16,2048]{2,1,0:T(8,128)S(1)}, f32[4,16,2048]{2,1,0:T(8,128)S(1)}, f32[4,16,2048]{2,1,0:T(8,128)S(1)}) custom-call(f32[16,4,2048]{2,1,0:T(4,128)} %u_ref.1, f32[16,4,2048]{2,1,0:T(4,128)} %m_ref.1, s32[16,2048]{1,0:T(8,128)} %ice_hbm.1, s32[4,16]{1,0:T(4,128)} %bitcast.3, f32[4,8,16]{2,1,0:T(8,128)} %bitcast.2, f32[8]{0:T(128)} %mu_hbm.1, ...), custom_call_target="tpu_custom_call" | custom-call | tf_op jit(solution)/shard_map/pallas_call | solution.py:759
  41.2 1.2 %shard_map.122 = (f32[16,4,2048]{2,1,0:T(4,128)}, f32[16,4,2048]{2,1,0:T(4,128)}, f32[16,4,2048]{2,1,0:T(4,128)}) custom-call(f32[4,16,2048]{2,1,0:T(8,128)S(1)} %get-tuple-element.6.refs_0_, f32[4,16,2048]{2,1,0:T(8,128)S(1)} %get-tuple-element.7.refs_1_, f32[4,16,2048]{2,1,0:T(8,128)S(1)} %get-tuple-element.8.refs_2_), custom_call_target="tpu_custom_call" | custom-call | tf_op jit(solution)/shard_map/pallas_call | solution.py:725

commit v4 on v3

--- a/solution.py
+++ b/solution.py
@@ -265,7 +265,7 @@
     weight = relax_factor / (6.0 + kappa_shift)
 
     def device(index):
-        return (index // rad_n, lax.rem(index, rad_n))
+        return (lax.div(index, rad_n), lax.rem(index, rad_n))
 
     def peer(d):
         return lax.rem(me + d, count)
@@ -312,9 +312,10 @@
         lax.fori_loop(1, count, start, 0)
 
     def each(src_of, dst, send_sem, recv_sem, how):
+        other = device(peer(1))
+
         def wait(d, carry):
-            q = peer(d)
-            copy = remote(src_of(q), dst.at[me], send_sem.at[d], recv_sem.at[d], device(q))
+            copy = remote(src_of(me), dst.at[me], send_sem.at[d], recv_sem.at[d], other)
             copy.wait_recv() if how == "recv" else copy.wait_send()
             return carry
 
@@ -354,20 +355,24 @@
         row = lax.broadcasted_iota(jnp.int32, (rows, nlon), 0)
 
         def forward(r, when):
-            @pl.when(jnp.logical_and(when, more))
+            if not more:
+                return
+
+            @pl.when(when)
             def _():
                 send_lat(s + 1, r)
 
-        def inner(r):
+        def arrived(r):
             for side, there, _, target in poles:
                 @pl.when(there)
                 def _():
                     lat_copy(s, 1 - side, r, target).wait_recv()
 
+        def inner(r, north, south):
             f, m = ubuf[s, r], m_out[r]
             beside = pltpu.roll(f, 1, 1) + pltpu.roll(f, nlon - 1, 1)
-            beside += jnp.where(row == 0, lat_in[s, 0, r], pltpu.roll(f, 1, 0))
-            beside += jnp.where(row == rows - 1, lat_in[s, 1, r], pltpu.roll(f, rows - 1, 0))
+            beside += jnp.where(row == 0, north, pltpu.roll(f, 1, 0))
+            beside += jnp.where(row == rows - 1, south, pltpu.roll(f, rows - 1, 0))
             if r > 0:
                 beside += ubuf[s, r - 1]
             if r < layers - 1:
@@ -376,15 +381,24 @@
             update = (sbuf[r] - m) * (weight / stiff) - relax_factor * f + weight * beside
             ubuf[s + 1, r] = f + update
             m_out[r] = decay_ref[r] * m + stiff * update
-            alone = True
-            for side, there, edge, _ in sides:
-                if edge == r:
-                    alone = jnp.logical_not(there)
-            forward(r, alone)
-
-        rest = list(range(1, layers - 1))
-        inner(layers - 1)
-        inner(0)
+
+        def middle(r):
+            arrived(r)
+            inner(r, lat_in[s, 0, r], lat_in[s, 1, r])
+            forward(r, True)
+
+        between = list(range(1, layers - 1))
+        edges = [(r, there) for _, there, r, _ in sides]
+        for r, _ in edges:
+            inner(r, 0.0, 0.0)
+        middle(between.pop(0))
+        for r, there in edges:
+            arrived(r)
+            for side, _, j, _ in poles:
+                extra = weight * lat_in[s, side, r]
+                ubuf[s + 1, r, j : j + 1, :] += extra
+                m_out[r, j : j + 1, :] += stiff_ref[r, j : j + 1, :] * extra
+            forward(r, jnp.logical_not(there))
         for k in range(CHUNKS):
             for side, there, r, target in sides:
                 @pl.when(there)
@@ -394,14 +408,10 @@
                     extra = weight * x_in[s, side, :, cols]
                     ubuf[s + 1, r, :, cols] += extra
                     m_out[r, :, cols] += stiff_ref[r] * extra
-                    if more is True:
+                    if more:
                         x_copy(s + 1, side, k, r, target).start()
-                    else:
-                        @pl.when(more)
-                        def _():
-                            x_copy(s + 1, side, k, r, target).start()
-            if k < len(rest):
-                inner(rest[k])
+            if k < len(between):
+                middle(between[k])
 
         for side, there, r, _ in sides:
             forward(r, there)
@@ -447,7 +457,7 @@
     for r in range(layers):
         pos = (rad * layers + (r + 1)).astype(f32) / total_rad
         sbuf[r] = (load_scale * pos) * ice
-    for load in loads[first:]:
+    for load in loads[first : first + 4]:
         load.wait()
 
     quarter = nlon // 4
@@ -593,6 +603,8 @@
 
     lax.fori_loop(0, 1, two, 0)
 
+    for load in loads[first + 4 :]:
+        load.wait()
     each(lambda q: pack_out.at[q], pack_in, a_send, a_recv, "recv")
     near = lax.broadcasted_iota(jnp.int32, (16, LANES), 1) < LANES // 2
     us, qs, ss = [], [], []
@@ -650,6 +662,8 @@
 
     lax.fori_loop(1, SWEEPS, two, 0)
 
+    each(lambda q: grav_ref, g_in, g_send, g_recv, "send")
+    each(lambda q: pack_out.at[q], pack_in, a_send, a_recv, "send")
     each(lambda q: back_out.at[q], back_in, b_send, b_recv, "recv")
     parts = swap_groups(
         [
@@ -677,15 +691,8 @@
         p_out[:, :, cols] = value
         sbuf[:, :, cols] += coupling * value
 
-    def rest(s, carry):
-        sweep(s, s + 1 < last)
-        return carry
-
-    lax.fori_loop(SWEEPS, last, rest, 0)
-    u_out[...] = ubuf[last]
-
-    each(lambda q: grav_ref, g_in, g_send, g_recv, "send")
-    each(lambda q: pack_out.at[q], pack_in, a_send, a_recv, "send")
+    lax.fori_loop(SWEEPS, last - 1, two, 0)
+
     each(lambda q: back_out.at[q], back_in, b_send, b_recv, "send")
 
     def drain(s, carry):
@@ -701,7 +708,10 @@
                     lat_copy(s, side, r, target).wait_send()
         return carry
 
-    lax.fori_loop(0, last, drain, 0)
+    lax.fori_loop(0, last - 1, drain, 0)
+    sweep(last - 1, False)
+    u_out[...] = ubuf[last]
+    drain(last - 1, 0)
 
 
 def deliver_kernel(*refs):

time: 43 us -> 42.5 us (0.988); the launches traced: 42.4 us -> 42.4 us
  no operation moved by 1% of the time
where the time goes in v4:
time: 42.5 us; the launch traced here: 42.4 us
  Pallas kernels  41.7 us (98%)
  between operations  0.64 us (2%)
    pallas_call x1, Pallas kernels, fused(): pl.pallas_call(fused_kernel, out_shape=[block] * 3, in_specs=[hbm] * len(...  40.5 us
    pallas_call x1, Pallas kernels, deliver(): pl.pallas_call(deliver_kernel, out_shape=[jax.ShapeDtypeStruct((rows, lay...  1.24 us

profile of v4, /device:TPU:0, one launch (start us, length us, event | category | flops | bytes accessed | tf_op | source)
XLA Modules:
  0.0 42.4 jit_solution(14319801165966494297)
XLA Ops:
  0.6 40.5 %shard_map.121 = (f32[4,16,2048]{2,1,0:T(8,128)S(1)}, f32[4,16,2048]{2,1,0:T(8,128)S(1)}, f32[4,16,2048]{2,1,0:T(8,128)S(1)}) custom-call(f32[16,4,2048]{2,1,0:T(4,128)} %u_ref.1, f32[16,4,2048]{2,1,0:T(4,128)} %m_ref.1, s32[16,2048]{1,0:T(8,128)} %ice_hbm.1, s32[4,16]{1,0:T(4,128)} %bitcast.3, f32[4,8,16]{2,1,0:T(8,128)} %bitcast.2, f32[8]{0:T(128)} %mu_hbm.1, ...), custom_call_target="tpu_custom_call" | custom-call | tf_op jit(solution)/shard_map/pallas_call | solution.py:769
  41.1 1.2 %shard_map.122 = (f32[16,4,2048]{2,1,0:T(4,128)}, f32[16,4,2048]{2,1,0:T(4,128)}, f32[16,4,2048]{2,1,0:T(4,128)}) custom-call(f32[4,16,2048]{2,1,0:T(8,128)S(1)} %get-tuple-element.6.refs_0_, f32[4,16,2048]{2,1,0:T(8,128)S(1)} %get-tuple-element.7.refs_1_, f32[4,16,2048]{2,1,0:T(8,128)S(1)} %get-tuple-element.8.refs_2_), custom_call_target="tpu_custom_call" | custom-call | tf_op jit(solution)/shard_map/pallas_call | solution.py:735
